TPU v7x, 128 devices: a whole 4x4x4 slice. The times are simulated.
128 devices in a mesh: section: 4 (over x), expert: 32 (over y, z, core).
Axes of the slice: x: 4, y: 4, z: 4, core: 2. Of those that a mesh axis runs over, the one named last changes fastest.
Arguments:
- section_inputs: bfloat16 [4, 3, 2048, 2048], P('section', None, 'expert'), may hold values from -6 to 6
- cotangent: bfloat16 [3, 2048, 2048], P(None, 'expert'), may hold values from -6 to 6
- expert_ids: int32 [4, 3, 2048, 2], P('section', None, 'expert'), may hold values from 0 to 31, all different within a row; in each aligned block of 64 rows (0 to 63, 64 to 127, ..., all dimensions but the last counted through in order) at most 6 rows name the same one
- route_weights: float32 [4, 3, 2048, 2], P('section', None, 'expert'), may hold values from 0.2 to 1
- w_gate: bfloat16 [4, 32, 2048, 512], P('section', 'expert'), may hold values from -0.125 to 0.125
- w_up: bfloat16 [4, 32, 2048, 512], P('section', 'expert'), may hold values from -0.125 to 0.125
- w_down: bfloat16 [4, 32, 512, 2048], P('section', 'expert'), may hold values from -0.25 to 0.25
Outputs:
- input_grads: bfloat16 [4, 3, 2048, 2048], P('section', None, 'expert')
- grad_gate: float32 [4, 32, 2048, 512], P('section', 'expert')
- grad_up: float32 [4, 32, 2048, 512], P('section', 'expert')
- precond_down: float32 [4, 32, 512, 2048], P('section', 'expert')
Inputs may be any that keep to these rules, and one draw needn't show every extreme that they name: `expert_ids`: each token names two different experts. In each aligned block of 64 rows (the rows of one device in one layer and micro-batch) no expert is named by more than 6 rows, a bound that some block reaches.
All inputs are finite; a program needn't handle non-finite values.
Results may differ from a plain program's by a relative error of at most 0.013.
Values may be sent and summed in bfloat16 or wider, within the bound.
No kernel may reach another device: no remote copies, remote signals or barrier semaphores. Data moves between devices by JAX's collectives and lax.ppermute only.
A program may use at most 192 MiB of HBM per device.

v0:
```python
import functools

import jax
import jax.numpy as jnp
from jax import lax
from jax.experimental import pallas as pl
from jax.experimental.pallas import tpu as pltpu
from jax.sharding import PartitionSpec as P

NS_ITERS = 5

damping = 0.1
epsilon = 1e-06

LANES = 128
F32 = jnp.float32
BF16 = jnp.bfloat16
VM = pltpu.VMEM
SM = pltpu.SMEM
PARAMS = pltpu.CompilerParams(vmem_limit_bytes=60 << 20)
LIMITS = {"root": 62000000, "dispatch": 55000000, "backward": 55000000, "combine": 54000000, "first": 53500000, "forward": 62000000}


def estimate(flops, moved):
    return pl.CostEstimate(flops=int(flops), bytes_accessed=int(moved), transcendentals=0)


def dot(a, b, ad, bd):
    return lax.dot_general(a, b, (((ad,), (bd,)), ((), ())), preferred_element_type=F32)


HBM = pltpu.HBM
ANY = pl.ANY


def lanes_of(part):
    return pl.ds(pl.multiple_of(part * LANES, LANES), LANES)


def fold_rows(flat_ref, cur_ref, rows, fold):
    def some(part, carry):
        cur_ref[pl.ds(part, rows, stride=fold), :] = flat_ref[:, lanes_of(part)].astype(F32)
        return carry

    lax.fori_loop(0, fold, some, 0)


def flatten_rows(cur_ref, flat_ref, rows, fold):
    def some(part, carry):
        flat_ref[:, lanes_of(part)] = cur_ref[pl.ds(part, rows, stride=fold), :].astype(BF16)
        return carry

    lax.fori_loop(0, fold, some, 0)


def widen(got_ref, cur_ref, group):
    count, depth, _ = got_ref.shape

    def some(step, carry):
        part = got_ref[pl.ds(step * group, group)].astype(F32)
        here = pl.ds(pl.multiple_of(step * group * depth, group * depth), group * depth)
        cur_ref[here, :] = part.reshape(group * depth, LANES)
        return carry

    lax.fori_loop(0, count // group, some, 0)


def narrow(cur_ref, out_ref, begin, end, size):
    def some(step, carry):
        here = pl.ds(pl.multiple_of(step * size, size), size)
        out_ref[here, :] = cur_ref[here, :].astype(BF16)
        return carry

    lax.fori_loop(begin // size, end // size, some, 0)


def load_current(info_ref, top_ref, inc_ref, flat_ref, buf_ref, cur_ref, sem, rows, fold):
    def from_top():
        copy = pltpu.make_async_copy(top_ref.at[info_ref[0]], flat_ref, sem)
        copy.start()
        copy.wait()
        fold_rows(flat_ref, cur_ref, rows, fold)

    def from_above():
        copy = pltpu.make_async_copy(inc_ref, buf_ref, sem)
        copy.start()
        copy.wait()
        cur_ref[...] = buf_ref[...].astype(F32)

    if inc_ref is None:
        from_top()
    elif top_ref is None:
        from_above()
    else:
        pl.when(info_ref[1] == 1)(from_top)
        pl.when(info_ref[1] == 0)(from_above)


def place_rows(
    src_ref, scale_ref, plain, base, first, count, fold, group, stride, offset, cur_ref, out_ref
):
    def some(step, carry):
        for part in range(group):
            place = step * group + part
            row = src_ref[base + place]
            factor = scale_ref[base + place]
            if plain:
                factor = jnp.where(factor > 0.0, 1.0, 0.0)
            tile = cur_ref[pl.ds(pl.multiple_of(row * fold, fold), fold), :]
            out_ref[pl.ds(pl.multiple_of((step * stride + offset + part) * fold, fold), fold), :] = (
                tile * factor
            ).astype(BF16)
        return carry

    lax.fori_loop(first // group, (first + count) // group, some, 0)


CHUNKS = 2


def dispatch_kernel(
    has_top, has_inc, plain, rows, slots, fold, group, info_ref, src_ref, scale_ref, *refs
):
    refs = list(refs)
    top_ref = refs.pop(0) if has_top else None
    inc_ref = refs.pop(0) if has_inc else None
    out_ref, flat_ref, buf_ref, cur_ref, put_ref, sems = refs
    load_current(info_ref, top_ref, inc_ref, flat_ref, buf_ref, cur_ref, sems.at[0], rows, fold)
    base = info_ref[0] * slots
    count = slots // CHUNKS
    copies = []
    for chunk in range(CHUNKS):
        place_rows(
            src_ref, scale_ref, plain, base, chunk * count, count, fold, group, group, 0,
            cur_ref, put_ref,
        )
        part = pl.ds(chunk * count * fold, count * fold)
        copies.append(
            pltpu.make_async_copy(put_ref.at[part], out_ref.at[part], sems.at[1 + chunk])
        )
        copies[-1].start()
    for copy in copies:
        copy.wait()


def dispatch(info, src, scale, top, inc, plain, rows, slots, fold, group):
    arrays = [value for value in (top, inc) if value is not None]
    return pl.pallas_call(
        functools.partial(
            dispatch_kernel, top is not None, inc is not None, plain, rows, slots, fold, group
        ),
        out_shape=jax.ShapeDtypeStruct((slots * fold, LANES), BF16),
        grid_spec=pltpu.PrefetchScalarGridSpec(
            num_scalar_prefetch=2,
            grid=(1,),
            in_specs=[pl.BlockSpec(memory_space=SM)]
            + [pl.BlockSpec(memory_space=HBM)] * (top is not None)
            + [pl.BlockSpec(memory_space=ANY)] * (inc is not None),
            out_specs=pl.BlockSpec(memory_space=HBM),
            scratch_shapes=[
                VM((rows, fold * LANES), BF16),
                VM((rows * fold, LANES), BF16),
                VM((rows * fold, LANES), F32),
                VM((slots * fold, LANES), BF16),
                pltpu.SemaphoreType.DMA((1 + CHUNKS,)),
            ],
        ),
        compiler_params=pltpu.CompilerParams(vmem_limit_bytes=LIMITS["dispatch"]),
        cost_estimate=estimate(1e6, 4e6),
        name="dispatch",
    )(info, src, scale, *arrays)


def first_kernel(rows, slots, fold, group, src_ref, scale_ref, x_ref, top_ref, out_ref, *rest):
    buf_x, buf_g, cur_x, cur_g, put_ref, sems = rest
    copies = [
        pltpu.make_async_copy(x_ref.at[0], buf_x, sems.at[0]),
        pltpu.make_async_copy(top_ref.at[0], buf_g, sems.at[1]),
    ]
    for copy in copies:
        copy.start()
    copies[0].wait()
    fold_rows(buf_x, cur_x, rows, fold)
    copies[1].wait()
    fold_rows(buf_g, cur_g, rows, fold)
    count = slots // CHUNKS
    copies = []
    for chunk in range(CHUNKS):
        for offset, plain, cur in ((0, True, cur_x), (group, False, cur_g)):
            place_rows(
                src_ref, scale_ref, plain, 0, chunk * count, count, fold, group, 2 * group, offset,
                cur, put_ref,
            )
        part = pl.ds(chunk * count * fold * 2, count * fold * 2)
        copies.append(
            pltpu.make_async_copy(put_ref.at[part], out_ref.at[part], sems.at[2 + chunk])
        )
        copies[-1].start()
    for copy in copies:
        copy.wait()


def first_dispatch(src, scale, x, top, rows, slots, fold, group):
    return pl.pallas_call(
        functools.partial(first_kernel, rows, slots, fold, group),
        out_shape=jax.ShapeDtypeStruct((2 * slots * fold, LANES), BF16),
        in_specs=[pl.BlockSpec(memory_space=SM)] * 2 + [pl.BlockSpec(memory_space=HBM)] * 2,
        out_specs=pl.BlockSpec(memory_space=HBM),
        scratch_shapes=[VM((rows, fold * LANES), BF16)] * 2
        + [VM((rows * fold, LANES), F32)] * 2
        + [VM((2 * slots * fold, LANES), BF16), pltpu.SemaphoreType.DMA((2 + CHUNKS,))],
        compiler_params=PARAMS,
        cost_estimate=estimate(1e6, 4e6),
        name="first_dispatch",
    )(src, scale, x, top)


def combine_kernel(has_top, has_inc, last, rows, fold, info_ref, slot_ref, *refs):
    refs = list(refs)
    top_ref = refs.pop(0) if has_top else None
    inc_ref = refs.pop(0) if has_inc else None
    came_hbm = refs.pop(0)
    if last:
        old_ref, flat_ref, top_buf, buf_ref, cur_ref, came_ref, sems = refs
    else:
        new_ref, top_buf, buf_ref, cur_ref, came_ref, sems = refs
    came_copy = pltpu.make_async_copy(came_hbm, came_ref, sems.at[1])
    came_copy.start()
    load_current(info_ref, top_ref, inc_ref, top_buf, buf_ref, cur_ref, sems.at[0], rows, fold)
    came_copy.wait()
    base = info_ref[0] * rows * 2

    def some(step, carry):
        for part in range(4):
            row = step * 4 + part
            first = slot_ref[base + 2 * row]
            second = slot_ref[base + 2 * row + 1]
            here = pl.ds(pl.multiple_of(row * fold, fold), fold)
            one = came_ref[pl.ds(pl.multiple_of(first * fold, fold), fold), :].astype(F32)
            two = came_ref[pl.ds(pl.multiple_of(second * fold, fold), fold), :].astype(F32)
            total = cur_ref[here, :] + (one + two)
            if last:
                cur_ref[here, :] = total
            else:
                buf_ref[here, :] = total.astype(BF16)
        return carry

    if not last:
        half = rows // 2
        copies = []
        for chunk in range(2):
            lax.fori_loop(chunk * half // 4, (chunk + 1) * half // 4, some, 0)
            part = pl.ds(chunk * half * fold, half * fold)
            copies.append(
                pltpu.make_async_copy(buf_ref.at[part], new_ref.at[part], sems.at[2 + chunk])
            )
            copies[-1].start()
        for copy in copies:
            copy.wait()
    else:
        lax.fori_loop(0, rows // 4, some, 0)
        unfold_rows(info_ref, cur_ref, old_ref, flat_ref, rows, fold)


def unfold_rows(info_ref, cur_ref, old_ref, flat_ref, rows, fold):
    @pl.when(info_ref[2] == 1)
    def _():
        flatten_rows(cur_ref, flat_ref.at[0], rows, fold)

    @pl.when(info_ref[2] == 0)
    def _():
        flat_ref[...] = old_ref[...]


def combine(info, slot, top, inc, came, rows, slots, fold, results=None):
    last = results is not None
    arrays = [value for value in (top, inc, came) if value is not None]
    specs = [pl.BlockSpec(memory_space=HBM)] * (top is not None)
    specs += [pl.BlockSpec(memory_space=ANY)] * (len(arrays) - len(specs))
    aliases = {}
    out_shape = jax.ShapeDtypeStruct((rows * fold, LANES), BF16)
    out_specs = pl.BlockSpec(memory_space=HBM)
    if last:
        block = pl.BlockSpec((1, rows, fold * LANES), lambda i, info, *_: (info[0], 0, 0))
        aliases = {2 + len(arrays): 0}
        out_shape = jax.ShapeDtypeStruct(results.shape, BF16)
        arrays, specs, out_specs = arrays + [results], specs + [block], block
    return pl.pallas_call(
        functools.partial(combine_kernel, top is not None, inc is not None, last, rows, fold),
        out_shape=out_shape,
        grid_spec=pltpu.PrefetchScalarGridSpec(
            num_scalar_prefetch=2,
            grid=(1,),
            in_specs=specs,
            out_specs=out_specs,
            scratch_shapes=[
                VM((rows, fold * LANES), BF16),
                VM((rows * fold, LANES), BF16),
                VM((rows * fold, LANES), F32),
                VM((slots * fold, LANES), BF16),
                pltpu.SemaphoreType.DMA((4,)),
            ],
        ),
        input_output_aliases=aliases,
        compiler_params=pltpu.CompilerParams(vmem_limit_bytes=LIMITS["combine"]),
        cost_estimate=estimate(1e6, 4e6),
        name="combine",
    )(info, slot, *arrays)


def keep_kernel(rows, fold, aliased, info_ref, new_ref, *refs):
    old_ref, flat_ref, cur_ref = refs if aliased else (None, *refs)
    cur_ref[...] = new_ref[...].astype(F32)
    if aliased:
        unfold_rows(info_ref, cur_ref, old_ref, flat_ref, rows, fold)
    else:
        flatten_rows(cur_ref, flat_ref.at[0], rows, fold)


def keep_rows(info, new, results, ticks, rows, fold):
    block = pl.BlockSpec((1, rows, fold * LANES), lambda i, info: (info[0], 0, 0))
    more = [] if results is None else [results]
    return pl.pallas_call(
        functools.partial(keep_kernel, rows, fold, results is not None),
        out_shape=jax.ShapeDtypeStruct((ticks, rows, fold * LANES), BF16),
        grid_spec=pltpu.PrefetchScalarGridSpec(
            num_scalar_prefetch=1,
            grid=(1,),
            in_specs=[pl.BlockSpec((rows * fold, LANES), lambda i, info: (0, 0))] + [block] * len(more),
            out_specs=block,
            scratch_shapes=[VM((rows * fold, LANES), F32)],
        ),
        input_output_aliases={2: 0} if more else {},
        compiler_params=PARAMS,
        cost_estimate=estimate(1e6, 1e6),
        name="keep_rows",
    )(info, new, *more)


def gradients_kernel(lead_ref, dg_ref, du_ref, xs_ref, gs_ref, gate_ref, up_ref, down_ref):
    rows_x = xs_ref[...]
    gate_ref[...] = dot(rows_x, dg_ref[...], 0, 0)
    up_ref[...] = dot(rows_x, du_ref[...], 0, 0)
    down_ref[...] = dot(lead_ref[...], gs_ref[...], 1, 0)


def gradients(lead, dg, du, xs, gs):
    depth, width = xs.shape
    hidden = dg.shape[1]
    wide = 256

    def whole(value):
        return pl.BlockSpec(value.shape, lambda i: (0, 0))

    columns = pl.BlockSpec((depth, wide), lambda i: (0, i))
    rows_out = pl.BlockSpec((wide, hidden), lambda i: (i, 0))
    return pl.pallas_call(
        gradients_kernel,
        out_shape=(
            jax.ShapeDtypeStruct((width, hidden), F32),
            jax.ShapeDtypeStruct((width, hidden), F32),
            jax.ShapeDtypeStruct((hidden, width), F32),
        ),
        grid=(width // wide,),
        in_specs=[whole(lead), whole(dg), whole(du), columns, columns],
        out_specs=(rows_out, rows_out, pl.BlockSpec((hidden, wide), lambda i: (0, i))),
        compiler_params=PARAMS,
        cost_estimate=estimate(6 * hidden * width * depth, 18e6),
        name="gradients",
    )(lead, dg, du, xs, gs)


def forward_kernel(aliased, tick, slots, fold, experts, got_hbm, wg_hbm, wu_hbm, *refs):
    refs = list(refs)
    if aliased:
        refs.pop(0)
    xs_hbm, hid_hbm, fac_hbm, got, both_w, scr, xs, hid, fac, sems = refs
    copies = [
        pltpu.make_async_copy(got_hbm.at[:, pl.ds(0, got.shape[1])], got, sems.at[0]),
        pltpu.make_async_copy(wg_hbm, both_w.at[0], sems.at[1]),
        pltpu.make_async_copy(wu_hbm, both_w.at[1], sems.at[2]),
    ]
    for copy in copies:
        copy.start()
    copies[0].wait()
    widen(got, scr, 4)
    flatten_rows(scr, xs, slots, fold)
    puts = [
        pltpu.make_async_copy(xs, xs_hbm.at[pl.ds(tick * slots, slots)], sems.at[3]),
        pltpu.make_async_copy(hid, hid_hbm, sems.at[4]),
        pltpu.make_async_copy(fac, fac_hbm, sems.at[5]),
    ]
    puts[0].start()
    copies[1].wait()
    copies[2].wait()

    def project(which, carry):
        fac[which] = dot(xs[...], both_w[which], 1, 0)
        return carry

    lax.fori_loop(0, 2, project, 0)
    gate, up = fac[0], fac[1]
    logistic = jax.nn.sigmoid(gate)
    soft = gate * logistic
    fac[0] = up * (logistic * (1.0 + gate * (1.0 - logistic)))
    fac[1] = soft
    puts[2].start()
    hid[...] = (soft * up).astype(BF16)
    puts[1].start()
    for put in puts:
        put.wait()


def forward(got, wg, wu, xs_all, tick, ticks, slots, fold, limit):
    experts = got.shape[0]
    width, hidden = wg.shape
    arrays = [got, wg, wu]
    aliases = {}
    if xs_all is not None:
        arrays.append(xs_all)
        aliases = {3: 0}
    hbm_spec = pl.BlockSpec(memory_space=HBM)
    return pl.pallas_call(
        functools.partial(forward_kernel, xs_all is not None, tick, slots, fold, experts),
        out_shape=(
            jax.ShapeDtypeStruct((ticks * slots, width), BF16),
            jax.ShapeDtypeStruct((slots, hidden), BF16),
            jax.ShapeDtypeStruct((2, slots, hidden), F32),
        ),
        in_specs=[pl.BlockSpec(memory_space=ANY)] + [hbm_spec] * (len(arrays) - 1),
        out_specs=(hbm_spec,) * 3,
        scratch_shapes=[
            VM((experts, slots * fold // experts, LANES), BF16),
            VM((2, width, hidden), BF16),
            VM((slots * fold, LANES), F32),
            VM((slots, width), BF16),
            VM((slots, hidden), BF16),
            VM((2, slots, hidden), F32),
            pltpu.SemaphoreType.DMA((6,)),
        ],
        input_output_aliases=aliases,
        compiler_params=pltpu.CompilerParams(vmem_limit_bytes=limit),
        cost_estimate=estimate(4 * slots * width * hidden, 8e6),
        name="forward",
    )(*arrays)


def backward_kernel(
    aliased, count, slots, fold, info_ref, got_hbm, wd_hbm, wg_hbm, wu_hbm, *refs
):
    refs = list(refs)
    fac_hbm = refs[:count]
    del refs[:count]
    if aliased:
        del refs[:3]
    out_hbm, gs_hbm, dg_hbm, du_hbm, got, wd, wg, wu, fac, scr, gs, dg, du, out, sems = refs
    begin = got_hbm.shape[1] - got.shape[1]
    copies = [
        pltpu.make_async_copy(got_hbm.at[:, pl.ds(begin, got.shape[1])], got, sems.at[0]),
        pltpu.make_async_copy(wd_hbm, wd, sems.at[1]),
        pltpu.make_async_copy(wg_hbm, wg, sems.at[2]),
        pltpu.make_async_copy(wu_hbm, wu, sems.at[3]),
    ]
    copies[0].start()
    copies[1].start()
    for which in range(count):

        @pl.when(info_ref[0] == which)
        def _(which=which):
            pltpu.make_async_copy(fac_hbm[which], fac, sems.at[4]).start()

    copies[2].start()
    copies[3].start()
    copies[0].wait()
    widen(got, scr, 4)
    flatten_rows(scr, gs, slots, fold)
    mine = pl.ds(pl.multiple_of(info_ref[0] * slots, slots), slots)
    keeps = [
        pltpu.make_async_copy(gs, gs_hbm.at[mine], sems.at[5]),
        pltpu.make_async_copy(dg, dg_hbm.at[mine], sems.at[6]),
        pltpu.make_async_copy(du, du_hbm.at[mine], sems.at[7]),
    ]
    copies[1].wait()
    grad_hidden = dot(gs[...], wd[...], 1, 1)
    pltpu.make_async_copy(fac_hbm[0], fac, sems.at[4]).wait()
    d_gate = (grad_hidden * fac[0]).astype(BF16)
    d_up = (grad_hidden * fac[1]).astype(BF16)
    dg[...] = d_gate
    du[...] = d_up
    copies[2].wait()
    copies[3].wait()

    @pl.when(info_ref[2] == 1)
    def _():
        for keep in keeps:
            keep.start()

    puts = []
    wide = 4
    for part in range(0, fold, wide):
        cols = slice(part * LANES, (part + wide) * LANES)
        back = dot(d_gate, wg[cols, :], 1, 1) + dot(d_up, wu[cols, :], 1, 1)
        for inner in range(wide):
            scr[pl.ds(part + inner, slots, stride=fold), :] = back[
                :, inner * LANES : (inner + 1) * LANES
            ]
    size = slots * fold // 2
    for chunk in range(2):
        some = pl.ds(chunk * size, size)
        narrow(scr, out, chunk * size, (chunk + 1) * size, 256)
        puts.append(pltpu.make_async_copy(out.at[some], out_hbm.at[some], sems.at[8 + chunk]))
        puts[-1].start()
    for put in puts:
        put.wait()

    @pl.when(info_ref[2] == 1)
    def _():
        for keep in keeps:
            keep.wait()


def backward(info, got, wd, wg, wu, facs, kept, ticks, slots, fold, limit):
    width, hidden = wg.shape
    experts = got.shape[0]
    hbm_spec = pl.BlockSpec(memory_space=HBM)
    arrays = [got, wd, wg, wu, *facs]
    aliases = {}
    if kept is not None:
        aliases = {1 + len(arrays) + i: 1 + i for i in range(3)}
        arrays += list(kept)
    return pl.pallas_call(
        functools.partial(backward_kernel, kept is not None, len(facs), slots, fold),
        out_shape=(
            jax.ShapeDtypeStruct((slots * fold, LANES), BF16),
            jax.ShapeDtypeStruct((ticks * slots, width), BF16),
            jax.ShapeDtypeStruct((ticks * slots, hidden), BF16),
            jax.ShapeDtypeStruct((ticks * slots, hidden), BF16),
        ),
        grid_spec=pltpu.PrefetchScalarGridSpec(
            num_scalar_prefetch=1,
            grid=(1,),
            in_specs=[pl.BlockSpec(memory_space=ANY)] + [hbm_spec] * (len(arrays) - 1),
            out_specs=(hbm_spec,) * 4,
            scratch_shapes=[
                VM((experts, slots * fold // experts, LANES), BF16),
                VM((hidden, width), BF16),
                VM((width, hidden), BF16),
                VM((width, hidden), BF16),
                VM((2, slots, hidden), F32),
                VM((slots * fold, LANES), F32),
                VM((slots, width), BF16),
                VM((slots, hidden), BF16),
                VM((slots, hidden), BF16),
                VM((slots * fold, LANES), BF16),
                pltpu.SemaphoreType.DMA((10,)),
            ],
        ),
        input_output_aliases=aliases,
        compiler_params=pltpu.CompilerParams(vmem_limit_bytes=limit),
        cost_estimate=estimate(6 * slots * width * hidden, 12e6),
        name="backward",
    )(info, *arrays)


def tables(ids, weights, experts, capacity):
    ticks, rows, top = ids.shape
    flat = ids.reshape(ticks, rows * top)
    order = jnp.arange(rows * top, dtype=jnp.int32)
    same = (flat[:, :, None] == flat[:, None, :]) & (order[None, :] < order[:, None])[None]
    target = flat * capacity + same.astype(jnp.int32).sum(axis=2)
    places = jnp.arange(experts * capacity, dtype=jnp.int32)
    chosen = places[None, :, None] == target[:, None, :]
    source = jnp.where(chosen, (order // top)[None, None, :], 0).sum(axis=2)
    scale = jnp.where(chosen, weights.reshape(ticks, 1, rows * top), 0.0).sum(axis=2)
    return target.reshape(-1), source.reshape(-1), scale.reshape(-1)


def split(value):
    high = value.astype(BF16)
    return high, (value - high.astype(F32)).astype(BF16)


def mul(a, b):
    a_high, a_low = split(a)
    b_high, b_low = split(b)
    return dot(a_high, b_high, 1, 0) + (dot(a_high, b_low, 1, 0) + dot(a_low, b_high, 1, 0))


def eye_like(value):
    rows = lax.broadcasted_iota(jnp.int32, value.shape, 0)
    return jnp.where(rows == lax.broadcasted_iota(jnp.int32, value.shape, 1), 1.0, 0.0)


def total_of(value):
    return jnp.sum(jnp.sum(value, axis=1, keepdims=True), axis=0, keepdims=True)


RES, FACTOR, CURRENT = 0, 1, 4


def root_turns(buf_ref, turns):
    def product(step, carry):
        right = jnp.where(step == 0, FACTOR, jnp.where(step == 3, CURRENT, step))
        to = jnp.where(step == 0, RES, step + 1)
        buf_ref[to] = mul(buf_ref[step], buf_ref[right])
        return carry

    def turn(_, carry):
        current = buf_ref[CURRENT]
        buf_ref[FACTOR] = (5.0 * eye_like(current) - current) * 0.25
        return lax.fori_loop(0, 4, product, carry)

    lax.fori_loop(0, turns, turn, 0)


def root_start_kernel(count, turns, *refs):
    state_ref, buf_ref = refs[count:]
    gram = None
    for ref in refs[:count]:
        term = dot(ref[...], ref[...], 0, 0)
        gram = term if gram is None else gram + term
    identity_m = eye_like(gram)
    ratio = gram.shape[0] / (total_of(gram * identity_m) + epsilon)
    curvature = gram * ratio + damping * identity_m
    frobenius = jnp.sqrt(total_of(curvature * curvature))
    buf_ref[CURRENT] = curvature * (1.0 / frobenius)
    buf_ref[RES] = identity_m * lax.rsqrt(jnp.sqrt(frobenius))
    root_turns(buf_ref, turns)
    state_ref[0] = buf_ref[RES]
    state_ref[1] = buf_ref[CURRENT]


def root_more_kernel(turns, state_in, state_ref, buf_ref):
    buf_ref[RES] = state_in[0]
    buf_ref[CURRENT] = state_in[1]
    root_turns(buf_ref, turns)
    state_ref[0] = buf_ref[RES]
    state_ref[1] = buf_ref[CURRENT]


def root_end_kernel(count, state_in, *refs):
    lead_ref, root_ref = refs[count:]
    current = state_in[1]
    root_ref[...] = mul(state_in[0], (5.0 * eye_like(current) - current) * 0.25)
    high, low = split(root_ref[...])
    width = refs[0].shape[0]
    for which, ref in enumerate(refs[:count]):
        lead = dot(high, ref[...], 1, 1) + dot(low, ref[...], 1, 1)
        lead_ref[:, which * width : (which + 1) * width] = lead.astype(BF16)


def root_call(kernel, name, out_shape, flops, scratch, *arrays):
    whole = pl.BlockSpec(memory_space=pltpu.VMEM)
    return pl.pallas_call(
        kernel,
        out_shape=out_shape,
        in_specs=[whole] * len(arrays),
        out_specs=whole,
        scratch_shapes=[scratch],
        compiler_params=pltpu.CompilerParams(vmem_limit_bytes=LIMITS["root"]),
        cost_estimate=estimate(flops, 4e6),
        name=name,
    )(*arrays)


def shards(section_inputs, cotangent, expert_ids, route_weights, w_gate, w_up, w_down):
    section = lax.axis_index("section")
    sections = lax.axis_size("section")
    experts = lax.axis_size("expert")
    _, ticks, rows, width = section_inputs.shape
    fold = width // LANES
    capacity = max(2, 3 * rows // experts)
    slots = experts * capacity
    wg, wu, wd = w_gate[0, 0], w_up[0, 0], w_down[0, 0]
    hidden = wg.shape[1]

    slot, src, scale = tables(expert_ids[0], route_weights[0], experts, capacity)
    x_rows = section_inputs[0]

    def exchange(value):
        return lax.all_to_all(
            value.reshape(experts, -1, LANES), "expert", split_axis=0, concat_axis=0, tiled=True
        )

    def send(info, tops, inc, plain):
        return exchange(dispatch(info, src, scale, tops, inc, plain, rows, slots, fold, capacity))

    steps = sections - 1 + ticks
    start = sections - 1 - section
    is_top = (section == sections - 1).astype(jnp.int32)
    infos = []
    for step in range(steps):
        offset = step - start
        active = ((offset >= 0) & (offset < ticks)).astype(jnp.int32)
        infos.append(jnp.stack([jnp.clip(offset, 0, ticks - 1), is_top, active]).astype(jnp.int32))

    xs_all, hiddens, facs = None, [], []
    pair = jax.ShapeDtypeStruct((2, hidden, hidden), F32)
    work = VM((5, hidden, hidden), F32)
    product = 6 * hidden**3

    def root_part(part, beside):
        if part == 0:
            kernel = functools.partial(root_start_kernel, ticks, 2)
            value = root_call(kernel, "root_start", pair, 8 * product, work, *hiddens)
        elif part == 1:
            kernel = functools.partial(root_more_kernel, NS_ITERS - 3)
            value = root_call(kernel, "root_more", pair, 8 * product, work, state)
        else:
            shape = jax.ShapeDtypeStruct((hidden, ticks * slots), BF16)
            kernel = functools.partial(root_end_kernel, ticks)
            one = VM((hidden, hidden), F32)
            value = root_call(kernel, "root_end", shape, 3 * product, one, state, *hiddens)
        return lax.optimization_barrier((beside, value))

    both = exchange(first_dispatch(src, scale, x_rows, cotangent, rows, slots, fold, capacity))
    got_x = {0: both}
    kept, results, inc = None, None, None
    for step in range(steps):
        info = infos[step]
        tops = cotangent if step < ticks else None
        got = send(info, tops, inc, False) if step else both
        limit = LIMITS["backward"] if step else LIMITS["first"]
        if step < ticks:
            xs_all, hid, fac = forward(got_x[step], wg, wu, xs_all, step, ticks, slots, fold, LIMITS["forward"] if step else limit)
            hiddens.append(hid)
            facs.append(fac)
        if step == ticks:
            got, state = root_part(1, got)
        sent, *kept = backward(info, got, wd, wg, wu, facs, kept, ticks, slots, fold, limit)
        came = exchange(sent).reshape(slots * fold, LANES)
        if step == ticks - 1:
            came, state = root_part(0, came)
        if step == ticks:
            came, lead = root_part(2, came)
        if step < steps - 1:
            new = combine(info, slot, tops, inc, came, rows, slots, fold)
            results = keep_rows(info, new, results, ticks, rows, fold)
            inc = lax.ppermute(new, "section", [(s, s - 1) for s in range(1, sections)])
            inc, results = lax.optimization_barrier((inc, results))
        else:
            results = combine(info, slot, tops, inc, came, rows, slots, fold, results)
        if step + 1 < ticks:
            got_x[step + 1] = send(jnp.array([step + 1, 1, 1], jnp.int32), x_rows, None, True)

    gs, dg, du = kept
    grad_gate, grad_up, precond = gradients(lead, dg, du, xs_all, gs)
    return (results[None], grad_gate[None, None], grad_up[None, None], precond[None, None])


def solution(mesh):
    return jax.shard_map(
        shards,
        mesh=mesh,
        in_specs=(
            P("section", None, "expert", None),
            P(None, "expert", None),
            P("section", None, "expert", None),
            P("section", None, "expert", None),
            P("section", "expert", None, None),
            P("section", "expert", None, None),
            P("section", "expert", None, None),
        ),
        out_specs=(
            P("section", None, "expert", None),
            P("section", "expert", None, None),
            P("section", "expert", None, None),
            P("section", "expert", None, None),
        ),
        check_vma=False,
    )
```

profile of v0, /device:TPU:1, one launch (start us, length us, event | category | flops | bytes accessed | tf_op | source)
XLA Modules:
  0.0 382.8 jit_solution(333716419191376027)
XLA Ops:
  4.5 4.6 %first_dispatch.1 = bf16[6144,128]{1,0:T(8,128)(2,1)} custom-call(s32[576]{0:T(1024)} %reshape.115.src_ref, f32[576]{0:T(1024)} %reshape.116.scale_ref, bf16[3,64,2048]{2,1,0:T(8,128)(2,1)} %bitcast.82, bf16[3,64,2048]{2,1,0:T(8,128)(2,1)} %refs_0_.9), custom_call_target="tpu_custom_call" | custom-call | flops 1000000 | bytes 4000000 | tf_op jit(solution)/shard_map/first_dispatch/pallas_call | solution.py:204
  9.1 9.6 %all-to-all-start = ((bf16[32,192,128]{2,1,0:T(8,128)(2,1)}), bf16[32,192,128]{2,1,0:T(8,128)(2,1)S(1)}, u32[]{:S(2)}, u32[]{:S(2)}) async-start(bf16[32,192,128]{2,1,0:T(8,128)(2,1)} %bitcast.85), calls=%async_computation | async-start | bytes 3145728 | tf_op jit(solution)/shard_map/all_to_all | solution.py:681
  18.8 22.6 %all-to-all-done.got_hbm = bf16[32,192,128]{2,1,0:T(8,128)(2,1)S(1)} async-done(((bf16[32,192,128]{2,1,0:T(8,128)(2,1)}), bf16[32,192,128]{2,1,0:T(8,128)(2,1)S(1)}, u32[]{:S(2)}, u32[]{:S(2)}) %all-to-all-start) | async-done | bytes 1572896 | tf_op jit(solution)/shard_map/all_to_all | solution.py:681
  41.4 4.8 %forward.3 = (bf16[576,2048]{1,0:T(8,128)(2,1)}, bf16[192,512]{1,0:T(8,128)(2,1)S(1)}, f32[2,192,512]{2,1,0:T(8,128)S(1)}) custom-call(bf16[32,192,128]{2,1,0:T(8,128)(2,1)S(1)} %all-to-all-done.got_hbm, bf16[2048,512]{1,0:T(8,128)(2,1)} %bitcast.57, bf16[2048,512]{1,0:T(8,128)(2,1)} %bitcast.66), custom_call_target="tpu_custom_call" | custom-call | flops 805306368 | bytes 8000000 | tf_op jit(solution)/shard_map/forward/pallas_call | solution.py:423
  46.9 6.4 %backward.6 = (bf16[3072,128]{1,0:T(8,128)(2,1)}, bf16[576,2048]{1,0:T(8,128)(2,1)}, bf16[576,512]{1,0:T(8,128)(2,1)S(1)}, bf16[576,512]{1,0:T(8,128)(2,1)S(1)}) custom-call(s32[3]{0:T(128)S(1)} %pad_add_fusion.5.info_ref, bf16[32,192,128]{2,1,0:T(8,128)(2,1)} %copy-done.6, bf16[512,2048]{1,0:T(8,128)(2,1)} %bitcast.75, bf16[2048,512]{1,0:T(8,128)(2,1)} %bitcast.58, ...), custom_call_target="tpu_custom_call" | custom-call | flops 1207959552 | bytes 12000000 | tf_op jit(solution)/shard_map/backward/pallas_call | solution.py:531
  53.4 4.2 %all-to-all-start.1 = ((bf16[32,96,128]{2,1,0:T(8,128)(2,1)}), bf16[32,96,128]{2,1,0:T(8,128)(2,1)S(1)}, u32[]{:S(2)}, u32[]{:S(2)}) async-start(bf16[32,96,128]{2,1,0:T(8,128)(2,1)} %bitcast.19), calls=%async_computation.1 | async-start | bytes 1572864 | tf_op jit(solution)/shard_map/all_to_all | solution.py:681
  57.6 4.0 %dispatch.8 = bf16[3072,128]{1,0:T(8,128)(2,1)} custom-call(s32[3]{0:T(128)S(1)} %call_exported.0.info_ref, s32[576]{0:T(1024)S(1)} %copy-done.13, f32[576]{0:T(1024)S(1)} %copy-done.12, bf16[3,64,2048]{2,1,0:T(8,128)(2,1)} %bitcast.83), custom_call_target="tpu_custom_call" | custom-call | flops 1000000 | bytes 4000000 | tf_op jit(solution)/shard_map/dispatch/pallas_call | solution.py:148
  61.6 10.3 %all-to-all-done.1 = bf16[32,96,128]{2,1,0:T(8,128)(2,1)S(1)} async-done(((bf16[32,96,128]{2,1,0:T(8,128)(2,1)}), bf16[32,96,128]{2,1,0:T(8,128)(2,1)S(1)}, u32[]{:S(2)}, u32[]{:S(2)}) %all-to-all-start.1) | async-done | bytes 786464 | tf_op jit(solution)/shard_map/all_to_all | solution.py:681
  71.9 4.4 %all-to-all-start.3 = ((bf16[32,96,128]{2,1,0:T(8,128)(2,1)}), bf16[32,96,128]{2,1,0:T(8,128)(2,1)}, u32[]{:S(2)}, u32[]{:S(2)}) async-start(bf16[32,96,128]{2,1,0:T(8,128)(2,1)} %bitcast.22), calls=%async_computation.3 | async-start | bytes 1572864 | tf_op jit(solution)/shard_map/all_to_all | solution.py:681
  76.7 1.7 combine.6.new_ref
  78.4 1.3 collective-permute-start
  79.8 2.7 keep_rows.5.refs_0_
  82.5 5.7 %collective-permute-done.refs_1_ = bf16[1024,128]{1,0:T(8,128)(2,1)S(1)} collective-permute-done((bf16[1024,128]{1,0:T(8,128)(2,1)S(1)}, bf16[1024,128]{1,0:T(8,128)(2,1)S(1)}, u32[]{:S(2)}, u32[]{:S(2)}) %collective-permute-start) | collective-permute-done | bytes 262176 | tf_op jit(solution)/shard_map/ppermute | solution.py:739
  88.2 2.6 dispatch.7
  90.8 7.6 %all-to-all-start.2 = ((bf16[32,96,128]{2,1,0:T(8,128)(2,1)}), bf16[32,96,128]{2,1,0:T(8,128)(2,1)S(1)}, u32[]{:S(2)}, u32[]{:S(2)}) async-start(bf16[32,96,128]{2,1,0:T(8,128)(2,1)} %bitcast.21), calls=%async_computation.2 | async-start | bytes 1572864 | tf_op jit(solution)/shard_map/all_to_all | solution.py:681
  98.5 4.9 %forward.4 = (bf16[576,2048]{1,0:T(8,128)(2,1)}, bf16[192,512]{1,0:T(8,128)(2,1)}, f32[2,192,512]{2,1,0:T(8,128)}) custom-call(bf16[32,96,128]{2,1,0:T(8,128)(2,1)} %all-to-all-done.3.got_hbm, bf16[2048,512]{1,0:T(8,128)(2,1)} %bitcast.59, bf16[2048,512]{1,0:T(8,128)(2,1)} %bitcast.68, ...), custom_call_target="tpu_custom_call", output_to_operand_aliasing={{0}: (3, {})} | custom-call | flops 805306368 | bytes 8000000 | tf_op jit(solution)/shard_map/forward/pallas_call | solution.py:423
  103.3 9.4 %all-to-all-done.2.got_hbm = bf16[32,96,128]{2,1,0:T(8,128)(2,1)S(1)} async-done(((bf16[32,96,128]{2,1,0:T(8,128)(2,1)}), bf16[32,96,128]{2,1,0:T(8,128)(2,1)S(1)}, u32[]{:S(2)}, u32[]{:S(2)}) %all-to-all-start.2) | async-done | bytes 786464 | tf_op jit(solution)/shard_map/all_to_all | solution.py:681
  113.6 6.6 %backward.7 = (bf16[3072,128]{1,0:T(8,128)(2,1)}, bf16[576,2048]{1,0:T(8,128)(2,1)}, bf16[576,512]{1,0:T(8,128)(2,1)S(1)}, bf16[576,512]{1,0:T(8,128)(2,1)S(1)}) custom-call(s32[3]{0:T(128)S(1)} %pad_add_fusion.4.info_ref, bf16[32,96,128]{2,1,0:T(8,128)(2,1)} %copy-done.21, ...), custom_call_target="tpu_custom_call", output_to_operand_aliasing={{1}: (7, {}), {2}: (8, {}), {3}: (9, {})} | custom-call | flops 1207959552 | bytes 12000000 | tf_op jit(solution)/shard_map/backward/pallas_call | solution.py:531
  120.2 3.9 %all-to-all-start.4 = ((bf16[32,96,128]{2,1,0:T(8,128)(2,1)}), bf16[32,96,128]{2,1,0:T(8,128)(2,1)S(1)}, u32[]{:S(2)}, u32[]{:S(2)}) async-start(bf16[32,96,128]{2,1,0:T(8,128)(2,1)} %bitcast.89), calls=%async_computation.4 | async-start | bytes 1572864 | tf_op jit(solution)/shard_map/all_to_all | solution.py:681
  124.2 4.0 %dispatch.10 = bf16[3072,128]{1,0:T(8,128)(2,1)} custom-call(s32[3]{0:T(128)S(1)} %copy-done.19, s32[576]{0:T(1024)S(1)} %copy-done.13, f32[576]{0:T(1024)S(1)} %copy-done.12, bf16[3,64,2048]{2,1,0:T(8,128)(2,1)} %bitcast.84), custom_call_target="tpu_custom_call" | custom-call | flops 1000000 | bytes 4000000 | tf_op jit(solution)/shard_map/dispatch/pallas_call | solution.py:148
  128.2 10.2 %all-to-all-done.4 = bf16[32,96,128]{2,1,0:T(8,128)(2,1)S(1)} async-done(((bf16[32,96,128]{2,1,0:T(8,128)(2,1)}), bf16[32,96,128]{2,1,0:T(8,128)(2,1)S(1)}, u32[]{:S(2)}, u32[]{:S(2)}) %all-to-all-start.4) | async-done | bytes 786464 | tf_op jit(solution)/shard_map/all_to_all | solution.py:681
  138.4 4.4 %all-to-all-start.6 = ((bf16[32,96,128]{2,1,0:T(8,128)(2,1)}), bf16[32,96,128]{2,1,0:T(8,128)(2,1)}, u32[]{:S(2)}, u32[]{:S(2)}) async-start(bf16[32,96,128]{2,1,0:T(8,128)(2,1)} %bitcast.26), calls=%async_computation.6 | async-start | bytes 1572864 | tf_op jit(solution)/shard_map/all_to_all | solution.py:681
  142.8 1.4 combine.7.new_ref
  144.3 1.3 collective-permute-start.1
  145.7 2.5 keep_rows.6.refs_0_
  148.1 5.9 %collective-permute-done.1.refs_1_ = bf16[1024,128]{1,0:T(8,128)(2,1)S(1)} collective-permute-done((bf16[1024,128]{1,0:T(8,128)(2,1)S(1)}, bf16[1024,128]{1,0:T(8,128)(2,1)S(1)}, u32[]{:S(2)}, u32[]{:S(2)}) %collective-permute-start.1) | collective-permute-done | bytes 262176 | tf_op jit(solution)/shard_map/ppermute | solution.py:739
  154.0 2.6 dispatch.9
  156.9 7.5 %all-to-all-start.5 = ((bf16[32,96,128]{2,1,0:T(8,128)(2,1)}), bf16[32,96,128]{2,1,0:T(8,128)(2,1)S(1)}, u32[]{:S(2)}, u32[]{:S(2)}) async-start(bf16[32,96,128]{2,1,0:T(8,128)(2,1)} %bitcast.25), calls=%async_computation.5 | async-start | bytes 1572864 | tf_op jit(solution)/shard_map/all_to_all | solution.py:681
  164.4 4.8 %forward.5 = (bf16[576,2048]{1,0:T(8,128)(2,1)}, bf16[192,512]{1,0:T(8,128)(2,1)}, f32[2,192,512]{2,1,0:T(8,128)}) custom-call(bf16[32,96,128]{2,1,0:T(8,128)(2,1)} %all-to-all-done.6.got_hbm, bf16[2048,512]{1,0:T(8,128)(2,1)} %bitcast.61, bf16[2048,512]{1,0:T(8,128)(2,1)} %bitcast.70, ...), custom_call_target="tpu_custom_call", output_to_operand_aliasing={{0}: (3, {})} | custom-call | flops 805306368 | bytes 8000000 | tf_op jit(solution)/shard_map/forward/pallas_call | solution.py:423
  169.2 9.4 %all-to-all-done.5.got_hbm = bf16[32,96,128]{2,1,0:T(8,128)(2,1)S(1)} async-done(((bf16[32,96,128]{2,1,0:T(8,128)(2,1)}), bf16[32,96,128]{2,1,0:T(8,128)(2,1)S(1)}, u32[]{:S(2)}, u32[]{:S(2)}) %all-to-all-start.5) | async-done | bytes 786464 | tf_op jit(solution)/shard_map/all_to_all | solution.py:681
  179.5 6.6 %backward.8 = (bf16[3072,128]{1,0:T(8,128)(2,1)}, bf16[576,2048]{1,0:T(8,128)(2,1)}, bf16[576,512]{1,0:T(8,128)(2,1)S(1)}, bf16[576,512]{1,0:T(8,128)(2,1)S(1)}) custom-call(s32[3]{0:T(128)S(1)} %pad_add_fusion.3.info_ref, bf16[32,96,128]{2,1,0:T(8,128)(2,1)} %copy-done.22, ...), custom_call_target="tpu_custom_call", output_to_operand_aliasing={{1}: (8, {}), {2}: (9, {}), {3}: (10, {})} | custom-call | flops 1207959552 | bytes 12000000 | tf_op jit(solution)/shard_map/backward/pallas_call | solution.py:531
  186.1 3.8 all-to-all-start.7
  189.9 12.1 %root_start.1.state_in = f32[2,512,512]{2,1,0:T(8,128)} custom-call(bf16[192,512]{1,0:T(8,128)(2,1)} %copy-done.20, bf16[192,512]{1,0:T(8,128)(2,1)} %get-tuple-element.74.refs_1_, bf16[192,512]{1,0:T(8,128)(2,1)} %get-tuple-element.75.refs_2_), custom_call_target="tpu_custom_call" | custom-call | flops 6442450944 | bytes 4000000 | tf_op jit(solution)/shard_map/root_start/pallas_call | solution.py:654
  202.0 2.1 all-to-all-done.7
  204.2 1.4 combine.8.new_ref
  205.6 1.3 collective-permute-start.2
  207.0 2.5 keep_rows.7.refs_0_
  209.5 6.7 %collective-permute-done.2.refs_0_ = bf16[1024,128]{1,0:T(8,128)(2,1)S(1)} collective-permute-done((bf16[1024,128]{1,0:T(8,128)(2,1)S(1)}, bf16[1024,128]{1,0:T(8,128)(2,1)S(1)}, u32[]{:S(2)}, u32[]{:S(2)}) %collective-permute-start.2) | collective-permute-done | bytes 262176 | tf_op jit(solution)/shard_map/ppermute | solution.py:739
  216.2 2.6 dispatch.11
  218.8 5.4 %all-to-all-start.8 = ((bf16[32,96,128]{2,1,0:T(8,128)(2,1)}), bf16[32,96,128]{2,1,0:T(8,128)(2,1)S(1)}, u32[]{:S(2)}, u32[]{:S(2)}) async-start(bf16[32,96,128]{2,1,0:T(8,128)(2,1)} %bitcast.29), calls=%async_computation.8 | async-start | bytes 1572864 | tf_op jit(solution)/shard_map/all_to_all | solution.py:681
  224.2 11.5 %root_more.1.state_in = f32[2,512,512]{2,1,0:T(8,128)} custom-call(f32[2,512,512]{2,1,0:T(8,128)} %root_start.1.state_in), custom_call_target="tpu_custom_call" | custom-call | flops 6442450944 | bytes 4000000 | tf_op jit(solution)/shard_map/root_more/pallas_call | solution.py:654
  235.7 2.7 all-to-all-done.8.got_hbm
  239.3 7.1 %backward.9 = (bf16[3072,128]{1,0:T(8,128)(2,1)}, bf16[576,2048]{1,0:T(8,128)(2,1)}, bf16[576,512]{1,0:T(8,128)(2,1)S(1)}, bf16[576,512]{1,0:T(8,128)(2,1)S(1)}) custom-call(s32[3]{0:T(128)S(1)} %pad_add_fusion.2.info_ref, bf16[32,96,128]{2,1,0:T(8,128)(2,1)} %copy-done.23, ...), custom_call_target="tpu_custom_call", output_to_operand_aliasing={{1}: (8, {}), {2}: (9, {}), {3}: (10, {})} | custom-call | flops 1207959552 | bytes 12000000 | tf_op jit(solution)/shard_map/backward/pallas_call | solution.py:531
  246.4 4.7 %all-to-all-start.9 = ((bf16[32,96,128]{2,1,0:T(8,128)(2,1)}), bf16[32,96,128]{2,1,0:T(8,128)(2,1)S(1)}, u32[]{:S(2)}, u32[]{:S(2)}) async-start(bf16[32,96,128]{2,1,0:T(8,128)(2,1)} %bitcast.87), calls=%async_computation.9 | async-start | bytes 1572864 | tf_op jit(solution)/shard_map/all_to_all | solution.py:681
  251.1 4.9 %root_end.1.lead_ref = bf16[512,576]{1,0:T(8,128)(2,1)} custom-call(f32[2,512,512]{2,1,0:T(8,128)} %root_more.1.state_in, bf16[192,512]{1,0:T(8,128)(2,1)} %copy-done.20, bf16[192,512]{1,0:T(8,128)(2,1)} %get-tuple-element.74.refs_1_, bf16[192,512]{1,0:T(8,128)(2,1)} %get-tuple-element.75.refs_2_), custom_call_target="tpu_custom_call" | custom-call | flops 2415919104 | bytes 4000000 | tf_op jit(solution)/shard_map/root_end/pallas_call | solution.py:654
  256.0 9.3 %all-to-all-done.9 = bf16[32,96,128]{2,1,0:T(8,128)(2,1)S(1)} async-done(((bf16[32,96,128]{2,1,0:T(8,128)(2,1)}), bf16[32,96,128]{2,1,0:T(8,128)(2,1)S(1)}, u32[]{:S(2)}, u32[]{:S(2)}) %all-to-all-start.9) | async-done | bytes 786464 | tf_op jit(solution)/shard_map/all_to_all | solution.py:681
  265.3 1.4 combine.9.new_ref
  268.2 2.8 keep_rows.8.refs_0_
  271.0 5.7 %collective-permute-done.3.refs_0_ = bf16[1024,128]{1,0:T(8,128)(2,1)S(1)} collective-permute-done((bf16[1024,128]{1,0:T(8,128)(2,1)S(1)}, bf16[1024,128]{1,0:T(8,128)(2,1)S(1)}, u32[]{:S(2)}, u32[]{:S(2)}) %collective-permute-start.3) | collective-permute-done | bytes 262176 | tf_op jit(solution)/shard_map/ppermute | solution.py:739
  276.6 2.3 dispatch.12
  278.9 18.4 %all_to_all.70.got_hbm = bf16[32,96,128]{2,1,0:T(8,128)(2,1)} all-to-all(bf16[32,96,128]{2,1,0:T(8,128)(2,1)S(1)} %bitcast.56), channel_id=1, replica_groups=mesh['section'=4,'expert'=32] {'expert'}, dimensions={0} | all-to-all | bytes 1572864 | tf_op jit(solution)/shard_map/all_to_all | solution.py:681
  297.3 7.1 %backward.10 = (bf16[3072,128]{1,0:T(8,128)(2,1)}, bf16[576,2048]{1,0:T(8,128)(2,1)}, bf16[576,512]{1,0:T(8,128)(2,1)S(1)}, bf16[576,512]{1,0:T(8,128)(2,1)S(1)}) custom-call(s32[3]{0:T(128)S(1)} %pad_add_fusion.1.info_ref, bf16[32,96,128]{2,1,0:T(8,128)(2,1)} %all_to_all.70.got_hbm, ...), custom_call_target="tpu_custom_call", output_to_operand_aliasing={{1}: (8, {}), {2}: (9, {}), {3}: (10, {})} | custom-call | flops 1207959552 | bytes 12000000 | tf_op jit(solution)/shard_map/backward/pallas_call | solution.py:531
  304.4 18.0 %all_to_all.71 = bf16[32,96,128]{2,1,0:T(8,128)(2,1)S(1)} all-to-all(bf16[32,96,128]{2,1,0:T(8,128)(2,1)} %bitcast.90), channel_id=1, replica_groups=mesh['section'=4,'expert'=32] {'expert'}, dimensions={0} | all-to-all | bytes 1572864 | tf_op jit(solution)/shard_map/all_to_all | solution.py:681
  322.4 1.4 combine.10.new_ref
  323.9 1.3 collective-permute-start.4
  325.2 2.8 keep_rows.9.refs_2_
  328.1 5.7 %collective-permute-done.4.refs_0_ = bf16[1024,128]{1,0:T(8,128)(2,1)S(1)} collective-permute-done((bf16[1024,128]{1,0:T(8,128)(2,1)S(1)}, bf16[1024,128]{1,0:T(8,128)(2,1)S(1)}, u32[]{:S(2)}, u32[]{:S(2)}) %collective-permute-start.4) | collective-permute-done | bytes 262176 | tf_op jit(solution)/shard_map/ppermute | solution.py:739
  333.7 2.3 dispatch.13
  336.0 18.4 %all_to_all.72.got_hbm = bf16[32,96,128]{2,1,0:T(8,128)(2,1)} all-to-all(bf16[32,96,128]{2,1,0:T(8,128)(2,1)S(1)} %bitcast.55), channel_id=1, replica_groups=mesh['section'=4,'expert'=32] {'expert'}, dimensions={0} | all-to-all | bytes 1572864 | tf_op jit(solution)/shard_map/all_to_all | solution.py:681
  354.4 7.1 %backward.11 = (bf16[3072,128]{1,0:T(8,128)(2,1)}, bf16[576,2048]{1,0:T(8,128)(2,1)}, bf16[576,512]{1,0:T(8,128)(2,1)S(1)}, bf16[576,512]{1,0:T(8,128)(2,1)S(1)}) custom-call(s32[3]{0:T(128)S(1)} %pad_add_fusion.info_ref, bf16[32,96,128]{2,1,0:T(8,128)(2,1)} %all_to_all.72.got_hbm, ...), custom_call_target="tpu_custom_call", output_to_operand_aliasing={{1}: (8, {}), {2}: (9, {}), {3}: (10, {})} | custom-call | flops 1207959552 | bytes 12000000 | tf_op jit(solution)/shard_map/backward/pallas_call | solution.py:531
  361.5 3.8 all-to-all-start.13
  365.3 10.7 %gradients.1 = (f32[2048,512]{1,0:T(8,128)}, f32[2048,512]{1,0:T(8,128)}, f32[512,2048]{1,0:T(8,128)}) custom-call(bf16[512,576]{1,0:T(8,128)(2,1)} %root_end.1.lead_ref, bf16[576,512]{1,0:T(8,128)(2,1)} %copy-done.4, bf16[576,512]{1,0:T(8,128)(2,1)} %copy-done.5, bf16[576,2048]{1,0:T(8,128)(2,1)} %get-tuple-element.103.xs_ref, ...), custom_call_target="tpu_custom_call" | custom-call | flops 3623878656 | bytes 18000000 | tf_op jit(solution)/shard_map/gradients/pallas_call | solution.py:357
  376.0 3.5 all-to-all-done.13
  379.5 3.0 combine.11
  (76 shorter events, 9.5 us)
Async XLA Ops:
  9.1 32.3 %all-to-all-start = ((bf16[32,192,128]{2,1,0:T(8,128)(2,1)}), bf16[32,192,128]{2,1,0:T(8,128)(2,1)S(1)}, u32[]{:S(2)}, u32[]{:S(2)}) async-start(bf16[32,192,128]{2,1,0:T(8,128)(2,1)} %bitcast.85), calls=%async_computation | async-start | bytes 3145728 | tf_op jit(solution)/shard_map/all_to_all | solution.py:681
  18.8 57.9 %copy-start.18 = (s32[3]{0:T(128)}, s32[3]{0:T(128)S(1)}, u32[]{:S(2)}) copy-start(s32[3]{0:T(128)S(1)} %pad_add_fusion.5.info_ref) | copy-start | bytes 40
  41.4 4.9 %copy-start.6 = (bf16[32,192,128]{2,1,0:T(8,128)(2,1)}, bf16[32,192,128]{2,1,0:T(8,128)(2,1)S(1)}, u32[]{:S(2)}) copy-start(bf16[32,192,128]{2,1,0:T(8,128)(2,1)S(1)} %all-to-all-done.got_hbm) | copy-start | bytes 4718596
  46.2 0.7 copy-start.20
  46.9 6.4 %copy-start = (f32[2,192,512]{2,1,0:T(8,128)}, f32[2,192,512]{2,1,0:T(8,128)S(1)}, u32[]{:S(2)}) copy-start(f32[2,192,512]{2,1,0:T(8,128)S(1)} %get-tuple-element.56.refs_0_) | copy-start | bytes 2359300
  46.9 10.7 %copy-start.12 = (f32[576]{0:T(1024)S(1)}, f32[576]{0:T(1024)}, u32[]{:S(2)}) copy-start(f32[576]{0:T(1024)} %reshape.116.scale_ref) | copy-start | bytes 6916
  46.9 10.7 %copy-start.13 = (s32[576]{0:T(1024)S(1)}, s32[576]{0:T(1024)}, u32[]{:S(2)}) copy-start(s32[576]{0:T(1024)} %reshape.115.src_ref) | copy-start | bytes 6916
  53.3 23.0 %copy-start.24 = (s32[1,3,64,2]{2,3,1,0:T(2,128)S(1)}, s32[1,3,64,2]{2,3,1,0:T(2,128)}, u32[]{:S(2)}) copy-start(s32[1,3,64,2]{2,3,1,0:T(2,128)} %param.11) | copy-start | bytes 4612
  53.4 23.3 %copy-start.1 = (bf16[3,64,2048]{2,1,0:T(8,128)(2,1)S(1)}, bf16[3,64,2048]{2,1,0:T(8,128)(2,1)}, u32[]{:S(2)}) copy-start(bf16[3,64,2048]{2,1,0:T(8,128)(2,1)} %refs_0_.9) | copy-start | bytes 2359300
  53.4 18.6 %all-to-all-start.1 = ((bf16[32,96,128]{2,1,0:T(8,128)(2,1)}), bf16[32,96,128]{2,1,0:T(8,128)(2,1)S(1)}, u32[]{:S(2)}, u32[]{:S(2)}) async-start(bf16[32,96,128]{2,1,0:T(8,128)(2,1)} %bitcast.19), calls=%async_computation.1 | async-start | bytes 1572864 | tf_op jit(solution)/shard_map/all_to_all | solution.py:681
  71.9 18.9 %all-to-all-start.3 = ((bf16[32,96,128]{2,1,0:T(8,128)(2,1)}), bf16[32,96,128]{2,1,0:T(8,128)(2,1)}, u32[]{:S(2)}, u32[]{:S(2)}) async-start(bf16[32,96,128]{2,1,0:T(8,128)(2,1)} %bitcast.22), calls=%async_computation.3 | async-start | bytes 1572864 | tf_op jit(solution)/shard_map/all_to_all | solution.py:681
  78.4 1.4 copy-start.9
  78.4 9.8 %collective-permute-start = (bf16[1024,128]{1,0:T(8,128)(2,1)S(1)}, bf16[1024,128]{1,0:T(8,128)(2,1)S(1)}, u32[]{:S(2)}, u32[]{:S(2)}) collective-permute-start(bf16[1024,128]{1,0:T(8,128)(2,1)S(1)} %combine.6.new_ref), channel_id=1, source_target_pairs={{32,0},{64,32},{96,64},{33,1},{65,33},{97,65},{34,2},{66,34},{98,6... | collective-permute-start | bytes 786440 | tf_op jit(solution)/shard_map/ppermute | solution.py:739
  79.8 63.0 %copy-start.16 = (s32[3]{0:T(128)}, s32[3]{0:T(128)S(1)}, u32[]{:S(2)}) copy-start(s32[3]{0:T(128)S(1)} %pad_add_fusion.4.info_ref) | copy-start | bytes 40
  90.8 21.9 %all-to-all-start.2 = ((bf16[32,96,128]{2,1,0:T(8,128)(2,1)}), bf16[32,96,128]{2,1,0:T(8,128)(2,1)S(1)}, u32[]{:S(2)}, u32[]{:S(2)}) async-start(bf16[32,96,128]{2,1,0:T(8,128)(2,1)} %bitcast.21), calls=%async_computation.2 | async-start | bytes 1572864 | tf_op jit(solution)/shard_map/all_to_all | solution.py:681
  112.7 0.9 copy-start.21
  113.6 10.6 %copy-start.19 = (s32[3]{0:T(128)S(1)}, s32[3]{0:T(128)}, u32[]{:S(2)}) copy-start(s32[3]{0:T(128)} %constant.40.clone.info_ref) | copy-start | bytes 40
  120.2 22.6 %copy-start.2 = (bf16[3,64,2048]{2,1,0:T(8,128)(2,1)S(1)}, bf16[3,64,2048]{2,1,0:T(8,128)(2,1)}, u32[]{:S(2)}) copy-start(bf16[3,64,2048]{2,1,0:T(8,128)(2,1)} %refs_0_.9) | copy-start | bytes 2359300
  120.2 18.2 %all-to-all-start.4 = ((bf16[32,96,128]{2,1,0:T(8,128)(2,1)}), bf16[32,96,128]{2,1,0:T(8,128)(2,1)S(1)}, u32[]{:S(2)}, u32[]{:S(2)}) async-start(bf16[32,96,128]{2,1,0:T(8,128)(2,1)} %bitcast.89), calls=%async_computation.4 | async-start | bytes 1572864 | tf_op jit(solution)/shard_map/all_to_all | solution.py:681
  138.4 18.5 %all-to-all-start.6 = ((bf16[32,96,128]{2,1,0:T(8,128)(2,1)}), bf16[32,96,128]{2,1,0:T(8,128)(2,1)}, u32[]{:S(2)}, u32[]{:S(2)}) async-start(bf16[32,96,128]{2,1,0:T(8,128)(2,1)} %bitcast.26), calls=%async_computation.6 | async-start | bytes 1572864 | tf_op jit(solution)/shard_map/all_to_all | solution.py:681
  144.3 1.4 copy-start.10
  144.3 9.7 %collective-permute-start.1 = (bf16[1024,128]{1,0:T(8,128)(2,1)S(1)}, bf16[1024,128]{1,0:T(8,128)(2,1)S(1)}, u32[]{:S(2)}, u32[]{:S(2)}) collective-permute-start(bf16[1024,128]{1,0:T(8,128)(2,1)S(1)} %combine.7.new_ref), channel_id=1, source_target_pairs={{32,0},{64,32},{96,64},{33,1},{65,33},{97,65},{34,2},{66,34},{98,6... | collective-permute-start | bytes 786440 | tf_op jit(solution)/shard_map/ppermute | solution.py:739
  145.7 58.5 %copy-start.17 = (s32[3]{0:T(128)}, s32[3]{0:T(128)S(1)}, u32[]{:S(2)}) copy-start(s32[3]{0:T(128)S(1)} %pad_add_fusion.3.info_ref) | copy-start | bytes 40
  156.9 21.7 %all-to-all-start.5 = ((bf16[32,96,128]{2,1,0:T(8,128)(2,1)}), bf16[32,96,128]{2,1,0:T(8,128)(2,1)S(1)}, u32[]{:S(2)}, u32[]{:S(2)}) async-start(bf16[32,96,128]{2,1,0:T(8,128)(2,1)} %bitcast.25), calls=%async_computation.5 | async-start | bytes 1572864 | tf_op jit(solution)/shard_map/all_to_all | solution.py:681
  178.6 0.9 copy-start.22
  186.1 18.0 %all-to-all-start.7 = ((bf16[32,96,128]{2,1,0:T(8,128)(2,1)}), bf16[32,96,128]{2,1,0:T(8,128)(2,1)S(1)}, u32[]{:S(2)}, u32[]{:S(2)}) async-start(bf16[32,96,128]{2,1,0:T(8,128)(2,1)} %bitcast.88), calls=%async_computation.7 | async-start | bytes 1572864 | tf_op jit(solution)/shard_map/all_to_all | solution.py:681
  189.9 14.2 %copy-start.3 = (bf16[3,64,2048]{2,1,0:T(8,128)(2,1)S(1)}, bf16[3,64,2048]{2,1,0:T(8,128)(2,1)}, u32[]{:S(2)}) copy-start(bf16[3,64,2048]{2,1,0:T(8,128)(2,1)} %refs_0_.9) | copy-start | bytes 2359300
  205.6 1.4 copy-start.11
  205.6 10.6 %collective-permute-start.2 = (bf16[1024,128]{1,0:T(8,128)(2,1)S(1)}, bf16[1024,128]{1,0:T(8,128)(2,1)S(1)}, u32[]{:S(2)}, u32[]{:S(2)}) collective-permute-start(bf16[1024,128]{1,0:T(8,128)(2,1)S(1)} %combine.8.new_ref), channel_id=1, source_target_pairs={{32,0},{64,32},{96,64},{33,1},{65,33},{97,65},{34,2},{66,34},{98,6... | collective-permute-start | bytes 786440 | tf_op jit(solution)/shard_map/ppermute | solution.py:739
  207.0 58.3 %copy-start.14 = (s32[3]{0:T(128)}, s32[3]{0:T(128)S(1)}, u32[]{:S(2)}) copy-start(s32[3]{0:T(128)S(1)} %pad_add_fusion.2.info_ref) | copy-start | bytes 40
  218.8 19.6 %all-to-all-start.8 = ((bf16[32,96,128]{2,1,0:T(8,128)(2,1)}), bf16[32,96,128]{2,1,0:T(8,128)(2,1)S(1)}, u32[]{:S(2)}, u32[]{:S(2)}) async-start(bf16[32,96,128]{2,1,0:T(8,128)(2,1)} %bitcast.29), calls=%async_computation.8 | async-start | bytes 1572864 | tf_op jit(solution)/shard_map/all_to_all | solution.py:681
  238.4 0.9 copy-start.23
  246.4 18.9 %all-to-all-start.9 = ((bf16[32,96,128]{2,1,0:T(8,128)(2,1)}), bf16[32,96,128]{2,1,0:T(8,128)(2,1)S(1)}, u32[]{:S(2)}, u32[]{:S(2)}) async-start(bf16[32,96,128]{2,1,0:T(8,128)(2,1)} %bitcast.87), calls=%async_computation.9 | async-start | bytes 1572864 | tf_op jit(solution)/shard_map/all_to_all | solution.py:681
  266.8 1.4 copy-start.8
  266.8 9.8 %collective-permute-start.3 = (bf16[1024,128]{1,0:T(8,128)(2,1)S(1)}, bf16[1024,128]{1,0:T(8,128)(2,1)S(1)}, u32[]{:S(2)}, u32[]{:S(2)}) collective-permute-start(bf16[1024,128]{1,0:T(8,128)(2,1)S(1)} %combine.9.new_ref), channel_id=1, source_target_pairs={{32,0},{64,32},{96,64},{33,1},{65,33},{97,65},{34,2},{66,34},{98,6... | collective-permute-start | bytes 786440 | tf_op jit(solution)/shard_map/ppermute | solution.py:739
  268.2 54.3 %copy-start.15 = (s32[3]{0:T(128)}, s32[3]{0:T(128)S(1)}, u32[]{:S(2)}) copy-start(s32[3]{0:T(128)S(1)} %pad_add_fusion.1.info_ref) | copy-start | bytes 40
  323.8 1.4 copy-start.7
  323.9 9.8 %collective-permute-start.4 = (bf16[1024,128]{1,0:T(8,128)(2,1)S(1)}, bf16[1024,128]{1,0:T(8,128)(2,1)S(1)}, u32[]{:S(2)}, u32[]{:S(2)}) collective-permute-start(bf16[1024,128]{1,0:T(8,128)(2,1)S(1)} %combine.10.new_ref), channel_id=1, source_target_pairs={{32,0},{64,32},{96,64},{33,1},{65,33},{97,65},{34,2},{66,34},{98,6... | collective-permute-start | bytes 786440 | tf_op jit(solution)/shard_map/ppermute | solution.py:739
  361.5 3.8 copy-start.4
  361.5 3.8 copy-start.5
  361.5 18.0 %all-to-all-start.13 = ((bf16[32,96,128]{2,1,0:T(8,128)(2,1)}), bf16[32,96,128]{2,1,0:T(8,128)(2,1)S(1)}, u32[]{:S(2)}, u32[]{:S(2)}) async-start(bf16[32,96,128]{2,1,0:T(8,128)(2,1)} %bitcast.86), calls=%async_computation.13 | async-start | bytes 1572864 | tf_op jit(solution)/shard_map/all_to_all | solution.py:681
where the time goes:
time: 385 us; the launch traced here: 383 us
  Pallas kernels  143 us (37%)
  waiting for transfers between devices  109 us (28%)
  starting transfers between devices  65.8 us (17%)
  blocking collectives  54.9 us (14%)
  local copies, waits for them, and re-layouts  6.89 us (2%)
    all_to_all x11, waiting for transfers between devices, exchange(): lax.all_to_all(value.reshape(experts, -1, LANES), 'expert', split_axis=0,...  79.8 us
    all_to_all x11, starting transfers between devices, exchange(): lax.all_to_all(value.reshape(experts, -1, LANES), 'expert', split_axis=0,...  59.4 us
    all_to_all x3, blocking collectives, exchange(): lax.all_to_all(value.reshape(experts, -1, LANES), 'expert', split_axis=0,...  54.9 us
    pallas_call x6, Pallas kernels, backward(): pl.pallas_call(functools.partial(backward_kernel, kept is not None, len(f...  40.9 us
    ppermute x5, waiting for transfers between devices, shards(): inc = lax.ppermute(new, 'section', [(s, s - 1) for s in range(1, sections)])  29.6 us
    pallas_call x3, Pallas kernels, root_call(): pl.pallas_call(kernel, out_shape=out_shape, in_specs=[whole] * len(arrays...  28.5 us
    pallas_call x7, Pallas kernels, dispatch(): pl.pallas_call(functools.partial(dispatch_kernel, top is not None, inc is...  20.3 us
    pallas_call x3, Pallas kernels, forward(): pl.pallas_call(functools.partial(forward_kernel, xs_all is not None, tick...  14.5 us
  transfers between devices with their start and end apart: 16, of which 15 were waited for; matrix products, arithmetic and copies ran while one was open for 0% of the time, Pallas kernels for 20%

commit v1 on v0

--- a/solution.py
+++ b/solution.py
@@ -18,7 +18,7 @@
 VM = pltpu.VMEM
 SM = pltpu.SMEM
 PARAMS = pltpu.CompilerParams(vmem_limit_bytes=60 << 20)
-LIMITS = {"root": 62000000, "dispatch": 55000000, "backward": 55000000, "combine": 54000000, "first": 53500000, "forward": 62000000}
+LIMITS = {"root": 62000000, "dispatch": 55000000, "backward": 53500000, "combine": 54000000, "first": 53500000, "forward": 62000000}
 
 
 def estimate(flops, moved):
@@ -394,12 +394,16 @@
     copies[1].wait()
     copies[2].wait()
 
-    def project(which, carry):
-        fac[which] = dot(xs[...], both_w[which], 1, 0)
-        return carry
-
-    lax.fori_loop(0, 2, project, 0)
-    gate, up = fac[0], fac[1]
+    if tick == 0:
+        gate, up = dot(xs[...], both_w[0], 1, 0), dot(xs[...], both_w[1], 1, 0)
+    else:
+
+        def project(which, carry):
+            fac[which] = dot(xs[...], both_w[which], 1, 0)
+            return carry
+
+        lax.fori_loop(0, 2, project, 0)
+        gate, up = fac[0], fac[1]
     logistic = jax.nn.sigmoid(gate)
     soft = gate * logistic
     fac[0] = up * (logistic * (1.0 + gate * (1.0 - logistic)))
@@ -504,8 +508,8 @@
             scr[pl.ds(part + inner, slots, stride=fold), :] = back[
                 :, inner * LANES : (inner + 1) * LANES
             ]
-    size = slots * fold // 2
-    for chunk in range(2):
+    size = slots * fold // 4
+    for chunk in range(4):
         some = pl.ds(chunk * size, size)
         narrow(scr, out, chunk * size, (chunk + 1) * size, 256)
         puts.append(pltpu.make_async_copy(out.at[some], out_hbm.at[some], sems.at[8 + chunk]))
@@ -552,7 +556,7 @@
                 VM((slots, hidden), BF16),
                 VM((slots, hidden), BF16),
                 VM((slots * fold, LANES), BF16),
-                pltpu.SemaphoreType.DMA((10,)),
+                pltpu.SemaphoreType.DMA((12,)),
             ],
         ),
         input_output_aliases=aliases,
@@ -682,8 +686,8 @@
             value.reshape(experts, -1, LANES), "expert", split_axis=0, concat_axis=0, tiled=True
         )
 
-    def send(info, tops, inc, plain):
-        return exchange(dispatch(info, src, scale, tops, inc, plain, rows, slots, fold, capacity))
+    def pack(info, tops, inc, plain):
+        return dispatch(info, src, scale, tops, inc, plain, rows, slots, fold, capacity)
 
     steps = sections - 1 + ticks
     start = sections - 1 - section
@@ -719,29 +723,31 @@
     for step in range(steps):
         info = infos[step]
         tops = cotangent if step < ticks else None
-        got = send(info, tops, inc, False) if step else both
+        got = exchange(pack(info, tops, inc, False)) if step else both
         limit = LIMITS["backward"] if step else LIMITS["first"]
         if step < ticks:
             xs_all, hid, fac = forward(got_x[step], wg, wu, xs_all, step, ticks, slots, fold, LIMITS["forward"] if step else limit)
             hiddens.append(hid)
             facs.append(fac)
-        if step == ticks:
-            got, state = root_part(1, got)
         sent, *kept = backward(info, got, wd, wg, wu, facs, kept, ticks, slots, fold, limit)
         came = exchange(sent).reshape(slots * fold, LANES)
-        if step == ticks - 1:
-            came, state = root_part(0, came)
-        if step == ticks:
-            came, lead = root_part(2, came)
+        part = step - (ticks - 1)
+        if part in (0, 1):
+            came, state = root_part(part, came)
+        if part == 2:
+            came, lead = root_part(part, came)
         if step < steps - 1:
             new = combine(info, slot, tops, inc, came, rows, slots, fold)
+            if step + 1 < ticks:
+                more = pack(jnp.array([step + 1, 1, 1], jnp.int32), x_rows, None, True)
+                new, more = lax.optimization_barrier((new, more))
             results = keep_rows(info, new, results, ticks, rows, fold)
             inc = lax.ppermute(new, "section", [(s, s - 1) for s in range(1, sections)])
             inc, results = lax.optimization_barrier((inc, results))
         else:
             results = combine(info, slot, tops, inc, came, rows, slots, fold, results)
         if step + 1 < ticks:
-            got_x[step + 1] = send(jnp.array([step + 1, 1, 1], jnp.int32), x_rows, None, True)
+            got_x[step + 1] = exchange(more)
 
     gs, dg, du = kept
     grad_gate, grad_up, precond = gradients(lead, dg, du, xs_all, gs)

time: 385 us -> 379 us (0.984)
  starting transfers between devices: 65.8 us -> 59.1 us
  waiting for transfers between devices: 109 us -> 113 us
    all_to_all x11, starting transfers between devices: 59.4 us -> 52.7 us  [exchange(): lax.all_to_all(value.reshape(experts, -1, LANES), 'expert', split_axis=0,...]
  transfers between devices with their start and end apart: 16 -> 16, of which waited for: 15 -> 16; matrix products, arithmetic and copies ran while one was open for 0% -> 0% of each run, Pallas kernels for 20% -> 20%
where the time goes in v1:
time: 379 us; the launch traced here: 377 us
  Pallas kernels  142 us (37%)
  waiting for transfers between devices  113 us (30%)
  starting transfers between devices  59.1 us (16%)
  blocking collectives  56.7 us (15%)
  local copies, waits for them, and re-layouts  4.47 us (1%)
    all_to_all x11, waiting for transfers between devices, exchange(): lax.all_to_all(value.reshape(experts, -1, LANES), 'expert', split_axis=0,...  83.4 us
    all_to_all x3, blocking collectives, exchange(): lax.all_to_all(value.reshape(experts, -1, LANES), 'expert', split_axis=0,...  56.7 us
    all_to_all x11, starting transfers between devices, exchange(): lax.all_to_all(value.reshape(experts, -1, LANES), 'expert', split_axis=0,...  52.7 us
    pallas_call x6, Pallas kernels, backward(): pl.pallas_call(functools.partial(backward_kernel, kept is not None, len(f...  40.4 us
    ppermute x5, waiting for transfers between devices, shards(): inc = lax.ppermute(new, 'section', [(s, s - 1) for s in range(1, sections)])  29.1 us
    pallas_call x3, Pallas kernels, root_call(): pl.pallas_call(kernel, out_shape=out_shape, in_specs=[whole] * len(arrays...  28.5 us
    pallas_call x7, Pallas kernels, dispatch(): pl.pallas_call(functools.partial(dispatch_kernel, top is not None, inc is...  20 us
    pallas_call x3, Pallas kernels, forward(): pl.pallas_call(functools.partial(forward_kernel, xs_all is not None, tick...  14.2 us
  transfers between devices with their start and end apart: 16, of which 16 were waited for; matrix products, arithmetic and copies ran while one was open for 0% of the time, Pallas kernels for 20%

profile of v1, /device:TPU:1, one launch (start us, length us, event | category | flops | bytes accessed | tf_op | source)
XLA Modules:
  0.0 377.4 jit_solution(14194331876486168060)
XLA Ops:
  4.5 4.6 %first_dispatch.1 = bf16[6144,128]{1,0:T(8,128)(2,1)} custom-call(s32[576]{0:T(1024)} %reshape.115.src_ref, f32[576]{0:T(1024)} %reshape.116.scale_ref, bf16[3,64,2048]{2,1,0:T(8,128)(2,1)} %bitcast.84, bf16[3,64,2048]{2,1,0:T(8,128)(2,1)} %refs_0_.9), custom_call_target="tpu_custom_call" | custom-call | flops 1000000 | bytes 4000000 | tf_op jit(solution)/shard_map/first_dispatch/pallas_call | solution.py:204
  9.1 9.6 %all-to-all-start = ((bf16[32,192,128]{2,1,0:T(8,128)(2,1)}), bf16[32,192,128]{2,1,0:T(8,128)(2,1)S(1)}, u32[]{:S(2)}, u32[]{:S(2)}) async-start(bf16[32,192,128]{2,1,0:T(8,128)(2,1)} %bitcast.87), calls=%async_computation | async-start | bytes 3145728 | tf_op jit(solution)/shard_map/all_to_all | solution.py:685
  18.8 22.6 %all-to-all-done.got_hbm = bf16[32,192,128]{2,1,0:T(8,128)(2,1)S(1)} async-done(((bf16[32,192,128]{2,1,0:T(8,128)(2,1)}), bf16[32,192,128]{2,1,0:T(8,128)(2,1)S(1)}, u32[]{:S(2)}, u32[]{:S(2)}) %all-to-all-start) | async-done | bytes 1572896 | tf_op jit(solution)/shard_map/all_to_all | solution.py:685
  41.4 4.5 %forward.3 = (bf16[576,2048]{1,0:T(8,128)(2,1)}, bf16[192,512]{1,0:T(8,128)(2,1)S(1)}, f32[2,192,512]{2,1,0:T(8,128)S(1)}) custom-call(bf16[32,192,128]{2,1,0:T(8,128)(2,1)S(1)} %all-to-all-done.got_hbm, bf16[2048,512]{1,0:T(8,128)(2,1)} %bitcast.59, bf16[2048,512]{1,0:T(8,128)(2,1)} %bitcast.68), custom_call_target="tpu_custom_call" | custom-call | flops 805306368 | bytes 8000000 | tf_op jit(solution)/shard_map/forward/pallas_call | solution.py:427
  45.9 6.4 %backward.6 = (bf16[3072,128]{1,0:T(8,128)(2,1)}, bf16[576,2048]{1,0:T(8,128)(2,1)}, bf16[576,512]{1,0:T(8,128)(2,1)S(1)}, bf16[576,512]{1,0:T(8,128)(2,1)S(1)}) custom-call(s32[3]{0:T(128)S(1)} %pad_add_fusion.5.info_ref, bf16[32,192,128]{2,1,0:T(8,128)(2,1)} %copy-done.6, bf16[512,2048]{1,0:T(8,128)(2,1)} %bitcast.77, bf16[2048,512]{1,0:T(8,128)(2,1)} %bitcast.60, ...), custom_call_target="tpu_custom_call" | custom-call | flops 1207959552 | bytes 12000000 | tf_op jit(solution)/shard_map/backward/pallas_call | solution.py:535
  52.4 4.3 %all-to-all-start.1 = ((bf16[32,96,128]{2,1,0:T(8,128)(2,1)}), bf16[32,96,128]{2,1,0:T(8,128)(2,1)S(1)}, u32[]{:S(2)}, u32[]{:S(2)}) async-start(bf16[32,96,128]{2,1,0:T(8,128)(2,1)} %bitcast.19), calls=%async_computation.1 | async-start | bytes 1572864 | tf_op jit(solution)/shard_map/all_to_all | solution.py:685
  57.0 4.0 %dispatch.7 = bf16[3072,128]{1,0:T(8,128)(2,1)} custom-call(s32[3]{0:T(128)S(1)} %call_exported.0.info_ref, s32[576]{0:T(1024)S(1)} %copy-done.14, f32[576]{0:T(1024)S(1)} %copy-done.13, bf16[3,64,2048]{2,1,0:T(8,128)(2,1)} %bitcast.85), custom_call_target="tpu_custom_call" | custom-call | flops 1000000 | bytes 4000000 | tf_op jit(solution)/shard_map/dispatch/pallas_call | solution.py:148
  61.0 10.0 %all-to-all-done.1 = bf16[32,96,128]{2,1,0:T(8,128)(2,1)S(1)} async-done(((bf16[32,96,128]{2,1,0:T(8,128)(2,1)}), bf16[32,96,128]{2,1,0:T(8,128)(2,1)S(1)}, u32[]{:S(2)}, u32[]{:S(2)}) %all-to-all-start.1) | async-done | bytes 786464 | tf_op jit(solution)/shard_map/all_to_all | solution.py:685
  71.0 1.7 combine.6.new_ref
  72.7 3.8 all-to-all-start.3
  77.9 2.7 keep_rows.5.refs_0_
  80.6 5.4 %collective-permute-done.refs_1_ = bf16[1024,128]{1,0:T(8,128)(2,1)S(1)} collective-permute-done((bf16[1024,128]{1,0:T(8,128)(2,1)S(1)}, bf16[1024,128]{1,0:T(8,128)(2,1)S(1)}, u32[]{:S(2)}, u32[]{:S(2)}) %collective-permute-start) | collective-permute-done | bytes 262176 | tf_op jit(solution)/shard_map/ppermute | solution.py:745
  86.0 2.6 dispatch.8
  88.6 2.1 all-to-all-done.3.got_hbm
  90.7 6.0 %all-to-all-start.2 = ((bf16[32,96,128]{2,1,0:T(8,128)(2,1)}), bf16[32,96,128]{2,1,0:T(8,128)(2,1)S(1)}, u32[]{:S(2)}, u32[]{:S(2)}) async-start(bf16[32,96,128]{2,1,0:T(8,128)(2,1)} %bitcast.21), calls=%async_computation.2 | async-start | bytes 1572864 | tf_op jit(solution)/shard_map/all_to_all | solution.py:685
  96.8 4.8 %forward.4 = (bf16[576,2048]{1,0:T(8,128)(2,1)}, bf16[192,512]{1,0:T(8,128)(2,1)}, f32[2,192,512]{2,1,0:T(8,128)}) custom-call(bf16[32,96,128]{2,1,0:T(8,128)(2,1)} %copy-done.22, bf16[2048,512]{1,0:T(8,128)(2,1)} %bitcast.61, bf16[2048,512]{1,0:T(8,128)(2,1)} %bitcast.70, bf16[576,2048]{1,0:T(8,128)(2,1)} %get-tuple-element.65.refs_0_), custom_call_target="tpu_custom_call", output_to_operand_aliasing={{0}: (3, {})} | custom-call | flops 805306368 | bytes 8000000 | tf_op jit(solution)/shard_map/forward/pallas_call | solution.py:427
  101.6 9.4 %all-to-all-done.2.got_hbm = bf16[32,96,128]{2,1,0:T(8,128)(2,1)S(1)} async-done(((bf16[32,96,128]{2,1,0:T(8,128)(2,1)}), bf16[32,96,128]{2,1,0:T(8,128)(2,1)S(1)}, u32[]{:S(2)}, u32[]{:S(2)}) %all-to-all-start.2) | async-done | bytes 786464 | tf_op jit(solution)/shard_map/all_to_all | solution.py:685
  111.0 6.7 %backward.7 = (bf16[3072,128]{1,0:T(8,128)(2,1)S(1)}, bf16[576,2048]{1,0:T(8,128)(2,1)}, bf16[576,512]{1,0:T(8,128)(2,1)S(1)}, bf16[576,512]{1,0:T(8,128)(2,1)S(1)}) custom-call(s32[3]{0:T(128)S(1)} %pad_add_fusion.4.info_ref, bf16[32,96,128]{2,1,0:T(8,128)(2,1)S(1)} %all-to-all-done.2.got_hbm, ...), custom_call_target="tpu_custom_call", output_to_operand_aliasing={{1}: (7, {}), {2}: (8, {}), {3}: (9, {})} | custom-call | flops 1207959552 | bytes 12000000 | tf_op jit(solution)/shard_map/backward/pallas_call | solution.py:535
  118.5 3.9 %all-to-all-start.4 = ((bf16[32,96,128]{2,1,0:T(8,128)(2,1)}), bf16[32,96,128]{2,1,0:T(8,128)(2,1)S(1)}, u32[]{:S(2)}, u32[]{:S(2)}) async-start(bf16[32,96,128]{2,1,0:T(8,128)(2,1)} %bitcast.58), calls=%async_computation.4 | async-start | bytes 1572864 | tf_op jit(solution)/shard_map/all_to_all | solution.py:685
  122.5 4.0 %dispatch.9 = bf16[3072,128]{1,0:T(8,128)(2,1)} custom-call(s32[3]{0:T(128)S(1)} %copy-done.20, s32[576]{0:T(1024)S(1)} %copy-done.14, f32[576]{0:T(1024)S(1)} %copy-done.13, bf16[3,64,2048]{2,1,0:T(8,128)(2,1)} %bitcast.86), custom_call_target="tpu_custom_call" | custom-call | flops 1000000 | bytes 4000000 | tf_op jit(solution)/shard_map/dispatch/pallas_call | solution.py:148
  126.5 10.2 %all-to-all-done.4 = bf16[32,96,128]{2,1,0:T(8,128)(2,1)S(1)} async-done(((bf16[32,96,128]{2,1,0:T(8,128)(2,1)}), bf16[32,96,128]{2,1,0:T(8,128)(2,1)S(1)}, u32[]{:S(2)}, u32[]{:S(2)}) %all-to-all-start.4) | async-done | bytes 786464 | tf_op jit(solution)/shard_map/all_to_all | solution.py:685
  136.7 1.4 combine.7.new_ref
  138.2 3.8 %all-to-all-start.6 = ((bf16[32,96,128]{2,1,0:T(8,128)(2,1)}), bf16[32,96,128]{2,1,0:T(8,128)(2,1)S(1)}, u32[]{:S(2)}, u32[]{:S(2)}) async-start(bf16[32,96,128]{2,1,0:T(8,128)(2,1)} %bitcast.26), calls=%async_computation.6 | async-start | bytes 1572864 | tf_op jit(solution)/shard_map/all_to_all | solution.py:685
  142.0 1.3 collective-permute-start.1
  143.4 2.5 keep_rows.6.refs_0_
  145.8 5.7 %collective-permute-done.1.refs_1_ = bf16[1024,128]{1,0:T(8,128)(2,1)S(1)} collective-permute-done((bf16[1024,128]{1,0:T(8,128)(2,1)S(1)}, bf16[1024,128]{1,0:T(8,128)(2,1)S(1)}, u32[]{:S(2)}, u32[]{:S(2)}) %collective-permute-start.1) | collective-permute-done | bytes 262176 | tf_op jit(solution)/shard_map/ppermute | solution.py:745
  151.5 2.6 dispatch.10
  154.1 2.1 all-to-all-done.6.got_hbm
  156.2 6.1 %all-to-all-start.5 = ((bf16[32,96,128]{2,1,0:T(8,128)(2,1)}), bf16[32,96,128]{2,1,0:T(8,128)(2,1)S(1)}, u32[]{:S(2)}, u32[]{:S(2)}) async-start(bf16[32,96,128]{2,1,0:T(8,128)(2,1)} %bitcast.25), calls=%async_computation.5 | async-start | bytes 1572864 | tf_op jit(solution)/shard_map/all_to_all | solution.py:685
  162.3 4.8 %forward.5 = (bf16[576,2048]{1,0:T(8,128)(2,1)}, bf16[192,512]{1,0:T(8,128)(2,1)}, f32[2,192,512]{2,1,0:T(8,128)}) custom-call(bf16[32,96,128]{2,1,0:T(8,128)(2,1)} %copy-done.23, bf16[2048,512]{1,0:T(8,128)(2,1)} %bitcast.63, bf16[2048,512]{1,0:T(8,128)(2,1)} %bitcast.72, bf16[576,2048]{1,0:T(8,128)(2,1)} %get-tuple-element.75.refs_0_), custom_call_target="tpu_custom_call", output_to_operand_aliasing={{0}: (3, {})} | custom-call | flops 805306368 | bytes 8000000 | tf_op jit(solution)/shard_map/forward/pallas_call | solution.py:427
  167.1 9.4 %all-to-all-done.5.got_hbm = bf16[32,96,128]{2,1,0:T(8,128)(2,1)S(1)} async-done(((bf16[32,96,128]{2,1,0:T(8,128)(2,1)}), bf16[32,96,128]{2,1,0:T(8,128)(2,1)S(1)}, u32[]{:S(2)}, u32[]{:S(2)}) %all-to-all-start.5) | async-done | bytes 786464 | tf_op jit(solution)/shard_map/all_to_all | solution.py:685
  176.5 6.4 %backward.8 = (bf16[3072,128]{1,0:T(8,128)(2,1)}, bf16[576,2048]{1,0:T(8,128)(2,1)}, bf16[576,512]{1,0:T(8,128)(2,1)S(1)}, bf16[576,512]{1,0:T(8,128)(2,1)S(1)}) custom-call(s32[3]{0:T(128)S(1)} %pad_add_fusion.3.info_ref, bf16[32,96,128]{2,1,0:T(8,128)(2,1)S(1)} %all-to-all-done.5.got_hbm, ...), custom_call_target="tpu_custom_call", output_to_operand_aliasing={{1}: (8, {}), {2}: (9, {}), {3}: (10, {})} | custom-call | flops 1207959552 | bytes 12000000 | tf_op jit(solution)/shard_map/backward/pallas_call | solution.py:535
  182.9 3.8 %all-to-all-start.7 = ((bf16[32,96,128]{2,1,0:T(8,128)(2,1)}), bf16[32,96,128]{2,1,0:T(8,128)(2,1)S(1)}, u32[]{:S(2)}, u32[]{:S(2)}) async-start(bf16[32,96,128]{2,1,0:T(8,128)(2,1)} %bitcast.27), calls=%async_computation.7 | async-start | bytes 1572864 | tf_op jit(solution)/shard_map/all_to_all | solution.py:685
  186.7 12.1 %root_start.1.state_in = f32[2,512,512]{2,1,0:T(8,128)} custom-call(bf16[192,512]{1,0:T(8,128)(2,1)} %copy-done.21, bf16[192,512]{1,0:T(8,128)(2,1)} %get-tuple-element.82.refs_1_, bf16[192,512]{1,0:T(8,128)(2,1)} %get-tuple-element.83.refs_2_), custom_call_target="tpu_custom_call" | custom-call | flops 6442450944 | bytes 4000000 | tf_op jit(solution)/shard_map/root_start/pallas_call | solution.py:658
  198.8 2.1 all-to-all-done.7
  201.0 1.4 combine.8.new_ref
  202.4 1.3 collective-permute-start.2
  203.8 2.5 keep_rows.7.refs_0_
  206.3 6.7 %collective-permute-done.2.refs_0_ = bf16[1024,128]{1,0:T(8,128)(2,1)S(1)} collective-permute-done((bf16[1024,128]{1,0:T(8,128)(2,1)S(1)}, bf16[1024,128]{1,0:T(8,128)(2,1)S(1)}, u32[]{:S(2)}, u32[]{:S(2)}) %collective-permute-start.2) | collective-permute-done | bytes 262176 | tf_op jit(solution)/shard_map/ppermute | solution.py:745
  213.0 2.3 dispatch.11
  215.3 19.4 %all_to_all.70.got_hbm = bf16[32,96,128]{2,1,0:T(8,128)(2,1)S(1)} all-to-all(bf16[32,96,128]{2,1,0:T(8,128)(2,1)S(1)} %bitcast.56), channel_id=1, replica_groups=mesh['section'=4,'expert'=32] {'expert'}, dimensions={0} | all-to-all | bytes 1572864 | tf_op jit(solution)/shard_map/all_to_all | solution.py:685
  234.7 6.9 %backward.9 = (bf16[3072,128]{1,0:T(8,128)(2,1)}, bf16[576,2048]{1,0:T(8,128)(2,1)}, bf16[576,512]{1,0:T(8,128)(2,1)S(1)}, bf16[576,512]{1,0:T(8,128)(2,1)S(1)}) custom-call(s32[3]{0:T(128)S(1)} %pad_add_fusion.2.info_ref, bf16[32,96,128]{2,1,0:T(8,128)(2,1)S(1)} %all_to_all.70.got_hbm, ...), custom_call_target="tpu_custom_call", output_to_operand_aliasing={{1}: (8, {}), {2}: (9, {}), {3}: (10, {})} | custom-call | flops 1207959552 | bytes 12000000 | tf_op jit(solution)/shard_map/backward/pallas_call | solution.py:535
  241.6 3.8 %all-to-all-start.9 = ((bf16[32,96,128]{2,1,0:T(8,128)(2,1)}), bf16[32,96,128]{2,1,0:T(8,128)(2,1)S(1)}, u32[]{:S(2)}, u32[]{:S(2)}) async-start(bf16[32,96,128]{2,1,0:T(8,128)(2,1)} %bitcast.30), calls=%async_computation.9 | async-start | bytes 1572864 | tf_op jit(solution)/shard_map/all_to_all | solution.py:685
  245.4 11.5 %root_more.1.state_in = f32[2,512,512]{2,1,0:T(8,128)} custom-call(f32[2,512,512]{2,1,0:T(8,128)} %root_start.1.state_in), custom_call_target="tpu_custom_call" | custom-call | flops 6442450944 | bytes 4000000 | tf_op jit(solution)/shard_map/root_more/pallas_call | solution.py:658
  256.9 2.7 all-to-all-done.9
  259.6 1.4 combine.9.new_ref
  262.4 2.8 keep_rows.8.refs_0_
  265.2 5.7 %collective-permute-done.3.refs_0_ = bf16[1024,128]{1,0:T(8,128)(2,1)S(1)} collective-permute-done((bf16[1024,128]{1,0:T(8,128)(2,1)S(1)}, bf16[1024,128]{1,0:T(8,128)(2,1)S(1)}, u32[]{:S(2)}, u32[]{:S(2)}) %collective-permute-start.3) | collective-permute-done | bytes 262176 | tf_op jit(solution)/shard_map/ppermute | solution.py:745
  270.9 2.3 dispatch.12
  273.1 19.1 %all_to_all.71.got_hbm = bf16[32,96,128]{2,1,0:T(8,128)(2,1)S(1)} all-to-all(bf16[32,96,128]{2,1,0:T(8,128)(2,1)S(1)} %bitcast.57), channel_id=1, replica_groups=mesh['section'=4,'expert'=32] {'expert'}, dimensions={0} | all-to-all | bytes 1572864 | tf_op jit(solution)/shard_map/all_to_all | solution.py:685
  292.2 7.1 %backward.10 = (bf16[3072,128]{1,0:T(8,128)(2,1)}, bf16[576,2048]{1,0:T(8,128)(2,1)}, bf16[576,512]{1,0:T(8,128)(2,1)S(1)}, bf16[576,512]{1,0:T(8,128)(2,1)S(1)}) custom-call(s32[3]{0:T(128)S(1)} %pad_add_fusion.1.info_ref, bf16[32,96,128]{2,1,0:T(8,128)(2,1)S(1)} %all_to_all.71.got_hbm, ...), custom_call_target="tpu_custom_call", output_to_operand_aliasing={{1}: (8, {}), {2}: (9, {}), {3}: (10, {})} | custom-call | flops 1207959552 | bytes 12000000 | tf_op jit(solution)/shard_map/backward/pallas_call | solution.py:535
  299.4 3.8 %all-to-all-start.11 = ((bf16[32,96,128]{2,1,0:T(8,128)(2,1)}), bf16[32,96,128]{2,1,0:T(8,128)(2,1)S(1)}, u32[]{:S(2)}, u32[]{:S(2)}) async-start(bf16[32,96,128]{2,1,0:T(8,128)(2,1)} %bitcast.33), calls=%async_computation.11 | async-start | bytes 1572864 | tf_op jit(solution)/shard_map/all_to_all | solution.py:685
  303.2 4.8 %root_end.1.lead_ref = bf16[512,576]{1,0:T(8,128)(2,1)} custom-call(f32[2,512,512]{2,1,0:T(8,128)} %root_more.1.state_in, bf16[192,512]{1,0:T(8,128)(2,1)} %copy-done.21, bf16[192,512]{1,0:T(8,128)(2,1)} %get-tuple-element.82.refs_1_, bf16[192,512]{1,0:T(8,128)(2,1)} %get-tuple-element.83.refs_2_), custom_call_target="tpu_custom_call" | custom-call | flops 2415919104 | bytes 4000000 | tf_op jit(solution)/shard_map/root_end/pallas_call | solution.py:658
  308.0 9.4 %all-to-all-done.11 = bf16[32,96,128]{2,1,0:T(8,128)(2,1)S(1)} async-done(((bf16[32,96,128]{2,1,0:T(8,128)(2,1)}), bf16[32,96,128]{2,1,0:T(8,128)(2,1)S(1)}, u32[]{:S(2)}, u32[]{:S(2)}) %all-to-all-start.11) | async-done | bytes 786464 | tf_op jit(solution)/shard_map/all_to_all | solution.py:685
  317.4 1.4 combine.10.new_ref
  320.2 2.8 keep_rows.9.refs_2_
  323.0 5.7 %collective-permute-done.4.refs_0_ = bf16[1024,128]{1,0:T(8,128)(2,1)S(1)} collective-permute-done((bf16[1024,128]{1,0:T(8,128)(2,1)S(1)}, bf16[1024,128]{1,0:T(8,128)(2,1)S(1)}, u32[]{:S(2)}, u32[]{:S(2)}) %collective-permute-start.4) | collective-permute-done | bytes 262176 | tf_op jit(solution)/shard_map/ppermute | solution.py:745
  328.7 2.3 dispatch.13
  330.9 18.2 %all_to_all.72.got_hbm = bf16[32,96,128]{2,1,0:T(8,128)(2,1)S(1)} all-to-all(bf16[32,96,128]{2,1,0:T(8,128)(2,1)S(1)} %bitcast.55), channel_id=1, replica_groups=mesh['section'=4,'expert'=32] {'expert'}, dimensions={0} | all-to-all | bytes 1572864 | tf_op jit(solution)/shard_map/all_to_all | solution.py:685
  349.2 6.9 %backward.11 = (bf16[3072,128]{1,0:T(8,128)(2,1)}, bf16[576,2048]{1,0:T(8,128)(2,1)}, bf16[576,512]{1,0:T(8,128)(2,1)S(1)}, bf16[576,512]{1,0:T(8,128)(2,1)S(1)}) custom-call(s32[3]{0:T(128)S(1)} %pad_add_fusion.info_ref, bf16[32,96,128]{2,1,0:T(8,128)(2,1)S(1)} %all_to_all.72.got_hbm, ...), custom_call_target="tpu_custom_call", output_to_operand_aliasing={{1}: (8, {}), {2}: (9, {}), {3}: (10, {})} | custom-call | flops 1207959552 | bytes 12000000 | tf_op jit(solution)/shard_map/backward/pallas_call | solution.py:535
  356.1 3.8 %all-to-all-start.13 = ((bf16[32,96,128]{2,1,0:T(8,128)(2,1)}), bf16[32,96,128]{2,1,0:T(8,128)(2,1)S(1)}, u32[]{:S(2)}, u32[]{:S(2)}) async-start(bf16[32,96,128]{2,1,0:T(8,128)(2,1)} %bitcast.36), calls=%async_computation.13 | async-start | bytes 1572864 | tf_op jit(solution)/shard_map/all_to_all | solution.py:685
  359.9 10.7 %gradients.1 = (f32[2048,512]{1,0:T(8,128)}, f32[2048,512]{1,0:T(8,128)}, f32[512,2048]{1,0:T(8,128)}) custom-call(bf16[512,576]{1,0:T(8,128)(2,1)} %root_end.1.lead_ref, bf16[576,512]{1,0:T(8,128)(2,1)} %copy-done.4, bf16[576,512]{1,0:T(8,128)(2,1)} %copy-done.5, bf16[576,2048]{1,0:T(8,128)(2,1)} %get-tuple-element.111.xs_ref, ...), custom_call_target="tpu_custom_call" | custom-call | flops 3623878656 | bytes 18000000 | tf_op jit(solution)/shard_map/gradients/pallas_call | solution.py:357
  370.6 3.5 all-to-all-done.13
  374.2 3.0 combine.11
  (80 shorter events, 9.4 us)
Async XLA Ops:
  2.8 6.3 %copy-start.24 = (s32[3,128]{1,0:T(4,128)}, s32[3,128]{1,0:T(4,128)S(1)}, u32[]{:S(2)}) copy-start(s32[3,128]{1,0:T(4,128)S(1)} %convert_reduce_fusion) | copy-start | bytes 4612
  9.1 32.3 %all-to-all-start = ((bf16[32,192,128]{2,1,0:T(8,128)(2,1)}), bf16[32,192,128]{2,1,0:T(8,128)(2,1)S(1)}, u32[]{:S(2)}, u32[]{:S(2)}) async-start(bf16[32,192,128]{2,1,0:T(8,128)(2,1)} %bitcast.87), calls=%async_computation | async-start | bytes 3145728 | tf_op jit(solution)/shard_map/all_to_all | solution.py:685
  18.8 52.2 %copy-start.19 = (s32[3]{0:T(128)}, s32[3]{0:T(128)S(1)}, u32[]{:S(2)}) copy-start(s32[3]{0:T(128)S(1)} %pad_add_fusion.5.info_ref) | copy-start | bytes 40
  41.4 4.5 %copy-start.6 = (bf16[32,192,128]{2,1,0:T(8,128)(2,1)}, bf16[32,192,128]{2,1,0:T(8,128)(2,1)S(1)}, u32[]{:S(2)}) copy-start(bf16[32,192,128]{2,1,0:T(8,128)(2,1)S(1)} %all-to-all-done.got_hbm) | copy-start | bytes 4718596
  45.9 6.5 %copy-start = (f32[2,192,512]{2,1,0:T(8,128)}, f32[2,192,512]{2,1,0:T(8,128)S(1)}, u32[]{:S(2)}) copy-start(f32[2,192,512]{2,1,0:T(8,128)S(1)} %get-tuple-element.60.refs_0_) | copy-start | bytes 2359300
  45.9 6.5 %copy-start.21 = (bf16[192,512]{1,0:T(8,128)(2,1)}, bf16[192,512]{1,0:T(8,128)(2,1)S(1)}, u32[]{:S(2)}) copy-start(bf16[192,512]{1,0:T(8,128)(2,1)S(1)} %get-tuple-element.81.refs_0_) | copy-start | bytes 589828
  45.9 10.7 %copy-start.26 = (s32[1,3,64,2]{2,3,1,0:T(2,128)S(1)}, s32[1,3,64,2]{2,3,1,0:T(2,128)}, u32[]{:S(2)}) copy-start(s32[1,3,64,2]{2,3,1,0:T(2,128)} %param.11) | copy-start | bytes 4612
  45.9 11.0 %copy-start.13 = (f32[576]{0:T(1024)S(1)}, f32[576]{0:T(1024)}, u32[]{:S(2)}) copy-start(f32[576]{0:T(1024)} %reshape.116.scale_ref) | copy-start | bytes 6916
  45.9 11.0 %copy-start.14 = (s32[576]{0:T(1024)S(1)}, s32[576]{0:T(1024)}, u32[]{:S(2)}) copy-start(s32[576]{0:T(1024)} %reshape.115.src_ref) | copy-start | bytes 6916
  52.4 8.6 %copy-start.25 = (s32[3,128]{1,0:T(4,128)S(1)}, s32[3,128]{1,0:T(4,128)}, u32[]{:S(2)}) copy-start(s32[3,128]{1,0:T(4,128)} %copy-done.24) | copy-start | bytes 4612
  52.4 18.6 %copy-start.1 = (bf16[3,64,2048]{2,1,0:T(8,128)(2,1)S(1)}, bf16[3,64,2048]{2,1,0:T(8,128)(2,1)}, u32[]{:S(2)}) copy-start(bf16[3,64,2048]{2,1,0:T(8,128)(2,1)} %refs_0_.9) | copy-start | bytes 2359300
  52.4 18.6 %all-to-all-start.1 = ((bf16[32,96,128]{2,1,0:T(8,128)(2,1)}), bf16[32,96,128]{2,1,0:T(8,128)(2,1)S(1)}, u32[]{:S(2)}, u32[]{:S(2)}) async-start(bf16[32,96,128]{2,1,0:T(8,128)(2,1)} %bitcast.19), calls=%async_computation.1 | async-start | bytes 1572864 | tf_op jit(solution)/shard_map/all_to_all | solution.py:685
  72.7 5.2 %copy-start.8 = (bf16[1024,128]{1,0:T(8,128)(2,1)}, bf16[1024,128]{1,0:T(8,128)(2,1)S(1)}, u32[]{:S(2)}) copy-start(bf16[1024,128]{1,0:T(8,128)(2,1)S(1)} %combine.6.new_ref) | copy-start | bytes 786436
  72.7 18.0 %all-to-all-start.3 = ((bf16[32,96,128]{2,1,0:T(8,128)(2,1)}), bf16[32,96,128]{2,1,0:T(8,128)(2,1)S(1)}, u32[]{:S(2)}, u32[]{:S(2)}) async-start(bf16[32,96,128]{2,1,0:T(8,128)(2,1)} %bitcast.22), calls=%async_computation.3 | async-start | bytes 1572864 | tf_op jit(solution)/shard_map/all_to_all | solution.py:685
  76.5 9.5 %collective-permute-start = (bf16[1024,128]{1,0:T(8,128)(2,1)S(1)}, bf16[1024,128]{1,0:T(8,128)(2,1)S(1)}, u32[]{:S(2)}, u32[]{:S(2)}) collective-permute-start(bf16[1024,128]{1,0:T(8,128)(2,1)S(1)} %combine.6.new_ref), channel_id=1, source_target_pairs={{32,0},{64,32},{96,64},{33,1},{65,33},{97,65},{34,2},{66,34},{98,6... | collective-permute-start | bytes 786440 | tf_op jit(solution)/shard_map/ppermute | solution.py:745
  77.9 58.8 %copy-start.17 = (s32[3]{0:T(128)}, s32[3]{0:T(128)S(1)}, u32[]{:S(2)}) copy-start(s32[3]{0:T(128)S(1)} %pad_add_fusion.4.info_ref) | copy-start | bytes 40
  90.7 6.1 %copy-start.22 = (bf16[32,96,128]{2,1,0:T(8,128)(2,1)}, bf16[32,96,128]{2,1,0:T(8,128)(2,1)S(1)}, u32[]{:S(2)}) copy-start(bf16[32,96,128]{2,1,0:T(8,128)(2,1)S(1)} %all-to-all-done.3.got_hbm) | copy-start | bytes 2359300
  90.7 20.3 %all-to-all-start.2 = ((bf16[32,96,128]{2,1,0:T(8,128)(2,1)}), bf16[32,96,128]{2,1,0:T(8,128)(2,1)S(1)}, u32[]{:S(2)}, u32[]{:S(2)}) async-start(bf16[32,96,128]{2,1,0:T(8,128)(2,1)} %bitcast.21), calls=%async_computation.2 | async-start | bytes 1572864 | tf_op jit(solution)/shard_map/all_to_all | solution.py:685
  111.0 11.5 %copy-start.20 = (s32[3]{0:T(128)S(1)}, s32[3]{0:T(128)}, u32[]{:S(2)}) copy-start(s32[3]{0:T(128)} %constant.40.clone.info_ref) | copy-start | bytes 40
  117.7 0.9 copy-start.12
  118.5 18.2 %copy-start.2 = (bf16[3,64,2048]{2,1,0:T(8,128)(2,1)S(1)}, bf16[3,64,2048]{2,1,0:T(8,128)(2,1)}, u32[]{:S(2)}) copy-start(bf16[3,64,2048]{2,1,0:T(8,128)(2,1)} %refs_0_.9) | copy-start | bytes 2359300
  118.5 18.2 %all-to-all-start.4 = ((bf16[32,96,128]{2,1,0:T(8,128)(2,1)}), bf16[32,96,128]{2,1,0:T(8,128)(2,1)S(1)}, u32[]{:S(2)}, u32[]{:S(2)}) async-start(bf16[32,96,128]{2,1,0:T(8,128)(2,1)} %bitcast.58), calls=%async_computation.4 | async-start | bytes 1572864 | tf_op jit(solution)/shard_map/all_to_all | solution.py:685
  138.1 5.2 %copy-start.10 = (bf16[1024,128]{1,0:T(8,128)(2,1)}, bf16[1024,128]{1,0:T(8,128)(2,1)S(1)}, u32[]{:S(2)}) copy-start(bf16[1024,128]{1,0:T(8,128)(2,1)S(1)} %combine.7.new_ref) | copy-start | bytes 786436
  138.2 18.0 %all-to-all-start.6 = ((bf16[32,96,128]{2,1,0:T(8,128)(2,1)}), bf16[32,96,128]{2,1,0:T(8,128)(2,1)S(1)}, u32[]{:S(2)}, u32[]{:S(2)}) async-start(bf16[32,96,128]{2,1,0:T(8,128)(2,1)} %bitcast.26), calls=%async_computation.6 | async-start | bytes 1572864 | tf_op jit(solution)/shard_map/all_to_all | solution.py:685
  142.0 9.5 %collective-permute-start.1 = (bf16[1024,128]{1,0:T(8,128)(2,1)S(1)}, bf16[1024,128]{1,0:T(8,128)(2,1)S(1)}, u32[]{:S(2)}, u32[]{:S(2)}) collective-permute-start(bf16[1024,128]{1,0:T(8,128)(2,1)S(1)} %combine.7.new_ref), channel_id=1, source_target_pairs={{32,0},{64,32},{96,64},{33,1},{65,33},{97,65},{34,2},{66,34},{98,6... | collective-permute-start | bytes 786440 | tf_op jit(solution)/shard_map/ppermute | solution.py:745
  143.4 57.6 %copy-start.18 = (s32[3]{0:T(128)}, s32[3]{0:T(128)S(1)}, u32[]{:S(2)}) copy-start(s32[3]{0:T(128)S(1)} %pad_add_fusion.3.info_ref) | copy-start | bytes 40
  156.2 6.1 %copy-start.23 = (bf16[32,96,128]{2,1,0:T(8,128)(2,1)}, bf16[32,96,128]{2,1,0:T(8,128)(2,1)S(1)}, u32[]{:S(2)}) copy-start(bf16[32,96,128]{2,1,0:T(8,128)(2,1)S(1)} %all-to-all-done.6.got_hbm) | copy-start | bytes 2359300
  156.2 20.3 %all-to-all-start.5 = ((bf16[32,96,128]{2,1,0:T(8,128)(2,1)}), bf16[32,96,128]{2,1,0:T(8,128)(2,1)S(1)}, u32[]{:S(2)}, u32[]{:S(2)}) async-start(bf16[32,96,128]{2,1,0:T(8,128)(2,1)} %bitcast.25), calls=%async_computation.5 | async-start | bytes 1572864 | tf_op jit(solution)/shard_map/all_to_all | solution.py:685
  182.9 18.0 %all-to-all-start.7 = ((bf16[32,96,128]{2,1,0:T(8,128)(2,1)}), bf16[32,96,128]{2,1,0:T(8,128)(2,1)S(1)}, u32[]{:S(2)}, u32[]{:S(2)}) async-start(bf16[32,96,128]{2,1,0:T(8,128)(2,1)} %bitcast.27), calls=%async_computation.7 | async-start | bytes 1572864 | tf_op jit(solution)/shard_map/all_to_all | solution.py:685
  186.7 14.2 %copy-start.3 = (bf16[3,64,2048]{2,1,0:T(8,128)(2,1)S(1)}, bf16[3,64,2048]{2,1,0:T(8,128)(2,1)}, u32[]{:S(2)}) copy-start(bf16[3,64,2048]{2,1,0:T(8,128)(2,1)} %refs_0_.9) | copy-start | bytes 2359300
  202.4 1.4 copy-start.11
  202.4 10.6 %collective-permute-start.2 = (bf16[1024,128]{1,0:T(8,128)(2,1)S(1)}, bf16[1024,128]{1,0:T(8,128)(2,1)S(1)}, u32[]{:S(2)}, u32[]{:S(2)}) collective-permute-start(bf16[1024,128]{1,0:T(8,128)(2,1)S(1)} %combine.8.new_ref), channel_id=1, source_target_pairs={{32,0},{64,32},{96,64},{33,1},{65,33},{97,65},{34,2},{66,34},{98,6... | collective-permute-start | bytes 786440 | tf_op jit(solution)/shard_map/ppermute | solution.py:745
  203.8 55.8 %copy-start.16 = (s32[3]{0:T(128)}, s32[3]{0:T(128)S(1)}, u32[]{:S(2)}) copy-start(s32[3]{0:T(128)S(1)} %pad_add_fusion.2.info_ref) | copy-start | bytes 40
  241.6 18.0 %all-to-all-start.9 = ((bf16[32,96,128]{2,1,0:T(8,128)(2,1)}), bf16[32,96,128]{2,1,0:T(8,128)(2,1)S(1)}, u32[]{:S(2)}, u32[]{:S(2)}) async-start(bf16[32,96,128]{2,1,0:T(8,128)(2,1)} %bitcast.30), calls=%async_computation.9 | async-start | bytes 1572864 | tf_op jit(solution)/shard_map/all_to_all | solution.py:685
  261.0 1.4 copy-start.9
  261.0 9.8 %collective-permute-start.3 = (bf16[1024,128]{1,0:T(8,128)(2,1)S(1)}, bf16[1024,128]{1,0:T(8,128)(2,1)S(1)}, u32[]{:S(2)}, u32[]{:S(2)}) collective-permute-start(bf16[1024,128]{1,0:T(8,128)(2,1)S(1)} %combine.9.new_ref), channel_id=1, source_target_pairs={{32,0},{64,32},{96,64},{33,1},{65,33},{97,65},{34,2},{66,34},{98,6... | collective-permute-start | bytes 786440 | tf_op jit(solution)/shard_map/ppermute | solution.py:745
  262.4 55.0 %copy-start.15 = (s32[3]{0:T(128)}, s32[3]{0:T(128)S(1)}, u32[]{:S(2)}) copy-start(s32[3]{0:T(128)S(1)} %pad_add_fusion.1.info_ref) | copy-start | bytes 40
  299.4 18.0 %all-to-all-start.11 = ((bf16[32,96,128]{2,1,0:T(8,128)(2,1)}), bf16[32,96,128]{2,1,0:T(8,128)(2,1)S(1)}, u32[]{:S(2)}, u32[]{:S(2)}) async-start(bf16[32,96,128]{2,1,0:T(8,128)(2,1)} %bitcast.33), calls=%async_computation.11 | async-start | bytes 1572864 | tf_op jit(solution)/shard_map/all_to_all | solution.py:685
  318.8 1.4 copy-start.7
  318.8 9.8 %collective-permute-start.4 = (bf16[1024,128]{1,0:T(8,128)(2,1)S(1)}, bf16[1024,128]{1,0:T(8,128)(2,1)S(1)}, u32[]{:S(2)}, u32[]{:S(2)}) collective-permute-start(bf16[1024,128]{1,0:T(8,128)(2,1)S(1)} %combine.10.new_ref), channel_id=1, source_target_pairs={{32,0},{64,32},{96,64},{33,1},{65,33},{97,65},{34,2},{66,34},{98,6... | collective-permute-start | bytes 786440 | tf_op jit(solution)/shard_map/ppermute | solution.py:745
  356.1 3.8 %copy-start.4 = (bf16[576,512]{1,0:T(8,128)(2,1)}, bf16[576,512]{1,0:T(8,128)(2,1)S(1)}, u32[]{:S(2)}) copy-start(bf16[576,512]{1,0:T(8,128)(2,1)S(1)} %get-tuple-element.109.dg_ref) | copy-start | bytes 1769476
  356.1 3.8 %copy-start.5 = (bf16[576,512]{1,0:T(8,128)(2,1)}, bf16[576,512]{1,0:T(8,128)(2,1)S(1)}, u32[]{:S(2)}) copy-start(bf16[576,512]{1,0:T(8,128)(2,1)S(1)} %get-tuple-element.110.du_ref) | copy-start | bytes 1769476
  356.1 18.0 %all-to-all-start.13 = ((bf16[32,96,128]{2,1,0:T(8,128)(2,1)}), bf16[32,96,128]{2,1,0:T(8,128)(2,1)S(1)}, u32[]{:S(2)}, u32[]{:S(2)}) async-start(bf16[32,96,128]{2,1,0:T(8,128)(2,1)} %bitcast.36), calls=%async_computation.13 | async-start | bytes 1572864 | tf_op jit(solution)/shard_map/all_to_all | solution.py:685

commit v2 on v1

--- a/solution.py
+++ b/solution.py
@@ -115,7 +115,8 @@
     lax.fori_loop(first // group, (first + count) // group, some, 0)
 
 
-CHUNKS = 2
+CHUNKS = 1
+FIRST_CHUNKS = 2
 
 
 def dispatch_kernel(
@@ -183,9 +184,9 @@
     fold_rows(buf_x, cur_x, rows, fold)
     copies[1].wait()
     fold_rows(buf_g, cur_g, rows, fold)
-    count = slots // CHUNKS
+    count = slots // FIRST_CHUNKS
     copies = []
-    for chunk in range(CHUNKS):
+    for chunk in range(FIRST_CHUNKS):
         for offset, plain, cur in ((0, True, cur_x), (group, False, cur_g)):
             place_rows(
                 src_ref, scale_ref, plain, 0, chunk * count, count, fold, group, 2 * group, offset,
@@ -208,7 +209,7 @@
         out_specs=pl.BlockSpec(memory_space=HBM),
         scratch_shapes=[VM((rows, fold * LANES), BF16)] * 2
         + [VM((rows * fold, LANES), F32)] * 2
-        + [VM((2 * slots * fold, LANES), BF16), pltpu.SemaphoreType.DMA((2 + CHUNKS,))],
+        + [VM((2 * slots * fold, LANES), BF16), pltpu.SemaphoreType.DMA((2 + FIRST_CHUNKS,))],
         compiler_params=PARAMS,
         cost_estimate=estimate(1e6, 4e6),
         name="first_dispatch",

time: 379 us -> 379 us (level)
  no operation moved by 1% of the time
where the time goes in v2:
time: 379 us; the launch traced here: 377 us
  Pallas kernels  141 us (37%)
  waiting for transfers between devices  112 us (30%)
  starting transfers between devices  59.4 us (16%)
  blocking collectives  56.8 us (15%)
  local copies, waits for them, and re-layouts  4.47 us (1%)
    all_to_all x11, waiting for transfers between devices, exchange(): lax.all_to_all(value.reshape(experts, -1, LANES), 'expert', split_axis=0,...  82.9 us
    all_to_all x3, blocking collectives, exchange(): lax.all_to_all(value.reshape(experts, -1, LANES), 'expert', split_axis=0,...  56.8 us
    all_to_all x11, starting transfers between devices, exchange(): lax.all_to_all(value.reshape(experts, -1, LANES), 'expert', split_axis=0,...  52.9 us
    pallas_call x6, Pallas kernels, backward(): pl.pallas_call(functools.partial(backward_kernel, kept is not None, len(f...  40.3 us
    ppermute x5, waiting for transfers between devices, shards(): inc = lax.ppermute(new, 'section', [(s, s - 1) for s in range(1, sections)])  29.1 us
    pallas_call x3, Pallas kernels, root_call(): pl.pallas_call(kernel, out_shape=out_shape, in_specs=[whole] * len(arrays...  28.5 us
    pallas_call x7, Pallas kernels, dispatch(): pl.pallas_call(functools.partial(dispatch_kernel, top is not None, inc is...  19.5 us
    pallas_call x3, Pallas kernels, forward(): pl.pallas_call(functools.partial(forward_kernel, xs_all is not None, tick...  14.2 us
  transfers between devices with their start and end apart: 16, of which 16 were waited for; matrix products, arithmetic and copies ran while one was open for 0% of the time, Pallas kernels for 20%

profile of v2, /device:TPU:1, one launch (start us, length us, event | category | flops | bytes accessed | tf_op | source)
XLA Modules:
  0.0 376.7 jit_solution(8238118259037549043)
XLA Ops:
  4.5 4.6 %first_dispatch.1 = bf16[6144,128]{1,0:T(8,128)(2,1)} custom-call(s32[576]{0:T(1024)} %reshape.115.src_ref, f32[576]{0:T(1024)} %reshape.116.scale_ref, bf16[3,64,2048]{2,1,0:T(8,128)(2,1)} %bitcast.84, bf16[3,64,2048]{2,1,0:T(8,128)(2,1)} %refs_0_.9), custom_call_target="tpu_custom_call" | custom-call | flops 1000000 | bytes 4000000 | tf_op jit(solution)/shard_map/first_dispatch/pallas_call | solution.py:205
  9.1 9.6 %all-to-all-start = ((bf16[32,192,128]{2,1,0:T(8,128)(2,1)}), bf16[32,192,128]{2,1,0:T(8,128)(2,1)S(1)}, u32[]{:S(2)}, u32[]{:S(2)}) async-start(bf16[32,192,128]{2,1,0:T(8,128)(2,1)} %bitcast.87), calls=%async_computation | async-start | bytes 3145728 | tf_op jit(solution)/shard_map/all_to_all | solution.py:686
  18.8 22.6 %all-to-all-done.got_hbm = bf16[32,192,128]{2,1,0:T(8,128)(2,1)S(1)} async-done(((bf16[32,192,128]{2,1,0:T(8,128)(2,1)}), bf16[32,192,128]{2,1,0:T(8,128)(2,1)S(1)}, u32[]{:S(2)}, u32[]{:S(2)}) %all-to-all-start) | async-done | bytes 1572896 | tf_op jit(solution)/shard_map/all_to_all | solution.py:686
  41.4 4.5 %forward.3 = (bf16[576,2048]{1,0:T(8,128)(2,1)}, bf16[192,512]{1,0:T(8,128)(2,1)S(1)}, f32[2,192,512]{2,1,0:T(8,128)S(1)}) custom-call(bf16[32,192,128]{2,1,0:T(8,128)(2,1)S(1)} %all-to-all-done.got_hbm, bf16[2048,512]{1,0:T(8,128)(2,1)} %bitcast.59, bf16[2048,512]{1,0:T(8,128)(2,1)} %bitcast.68), custom_call_target="tpu_custom_call" | custom-call | flops 805306368 | bytes 8000000 | tf_op jit(solution)/shard_map/forward/pallas_call | solution.py:428
  45.9 6.4 %backward.6 = (bf16[3072,128]{1,0:T(8,128)(2,1)}, bf16[576,2048]{1,0:T(8,128)(2,1)}, bf16[576,512]{1,0:T(8,128)(2,1)S(1)}, bf16[576,512]{1,0:T(8,128)(2,1)S(1)}) custom-call(s32[3]{0:T(128)S(1)} %pad_add_fusion.5.info_ref, bf16[32,192,128]{2,1,0:T(8,128)(2,1)} %copy-done.6, bf16[512,2048]{1,0:T(8,128)(2,1)} %bitcast.77, bf16[2048,512]{1,0:T(8,128)(2,1)} %bitcast.60, ...), custom_call_target="tpu_custom_call" | custom-call | flops 1207959552 | bytes 12000000 | tf_op jit(solution)/shard_map/backward/pallas_call | solution.py:536
  52.4 4.3 %all-to-all-start.1 = ((bf16[32,96,128]{2,1,0:T(8,128)(2,1)}), bf16[32,96,128]{2,1,0:T(8,128)(2,1)S(1)}, u32[]{:S(2)}, u32[]{:S(2)}) async-start(bf16[32,96,128]{2,1,0:T(8,128)(2,1)} %bitcast.19), calls=%async_computation.1 | async-start | bytes 1572864 | tf_op jit(solution)/shard_map/all_to_all | solution.py:686
  57.0 4.1 %dispatch.7 = bf16[3072,128]{1,0:T(8,128)(2,1)} custom-call(s32[3]{0:T(128)S(1)} %call_exported.0.info_ref, s32[576]{0:T(1024)S(1)} %copy-done.14, f32[576]{0:T(1024)S(1)} %copy-done.13, bf16[3,64,2048]{2,1,0:T(8,128)(2,1)} %bitcast.85), custom_call_target="tpu_custom_call" | custom-call | flops 1000000 | bytes 4000000 | tf_op jit(solution)/shard_map/dispatch/pallas_call | solution.py:149
  61.1 9.9 %all-to-all-done.1 = bf16[32,96,128]{2,1,0:T(8,128)(2,1)S(1)} async-done(((bf16[32,96,128]{2,1,0:T(8,128)(2,1)}), bf16[32,96,128]{2,1,0:T(8,128)(2,1)S(1)}, u32[]{:S(2)}, u32[]{:S(2)}) %all-to-all-start.1) | async-done | bytes 786464 | tf_op jit(solution)/shard_map/all_to_all | solution.py:686
  71.0 1.7 combine.6.new_ref
  72.7 3.8 %all-to-all-start.3 = ((bf16[32,96,128]{2,1,0:T(8,128)(2,1)}), bf16[32,96,128]{2,1,0:T(8,128)(2,1)S(1)}, u32[]{:S(2)}, u32[]{:S(2)}) async-start(bf16[32,96,128]{2,1,0:T(8,128)(2,1)} %bitcast.22), calls=%async_computation.3 | async-start | bytes 1572864 | tf_op jit(solution)/shard_map/all_to_all | solution.py:686
  76.5 1.3 collective-permute-start
  77.9 2.7 keep_rows.5.refs_0_
  80.6 5.4 %collective-permute-done.refs_1_ = bf16[1024,128]{1,0:T(8,128)(2,1)S(1)} collective-permute-done((bf16[1024,128]{1,0:T(8,128)(2,1)S(1)}, bf16[1024,128]{1,0:T(8,128)(2,1)S(1)}, u32[]{:S(2)}, u32[]{:S(2)}) %collective-permute-start) | collective-permute-done | bytes 262176 | tf_op jit(solution)/shard_map/ppermute | solution.py:746
  86.0 2.8 dispatch.8
  88.8 1.9 all-to-all-done.3.got_hbm
  90.7 6.2 %all-to-all-start.2 = ((bf16[32,96,128]{2,1,0:T(8,128)(2,1)}), bf16[32,96,128]{2,1,0:T(8,128)(2,1)S(1)}, u32[]{:S(2)}, u32[]{:S(2)}) async-start(bf16[32,96,128]{2,1,0:T(8,128)(2,1)} %bitcast.21), calls=%async_computation.2 | async-start | bytes 1572864 | tf_op jit(solution)/shard_map/all_to_all | solution.py:686
  96.9 4.9 %forward.4 = (bf16[576,2048]{1,0:T(8,128)(2,1)}, bf16[192,512]{1,0:T(8,128)(2,1)}, f32[2,192,512]{2,1,0:T(8,128)}) custom-call(bf16[32,96,128]{2,1,0:T(8,128)(2,1)} %copy-done.22, bf16[2048,512]{1,0:T(8,128)(2,1)} %bitcast.61, bf16[2048,512]{1,0:T(8,128)(2,1)} %bitcast.70, bf16[576,2048]{1,0:T(8,128)(2,1)} %get-tuple-element.65.refs_0_), custom_call_target="tpu_custom_call", output_to_operand_aliasing={{0}: (3, {})} | custom-call | flops 805306368 | bytes 8000000 | tf_op jit(solution)/shard_map/forward/pallas_call | solution.py:428
  101.8 9.4 %all-to-all-done.2.got_hbm = bf16[32,96,128]{2,1,0:T(8,128)(2,1)S(1)} async-done(((bf16[32,96,128]{2,1,0:T(8,128)(2,1)}), bf16[32,96,128]{2,1,0:T(8,128)(2,1)S(1)}, u32[]{:S(2)}, u32[]{:S(2)}) %all-to-all-start.2) | async-done | bytes 786464 | tf_op jit(solution)/shard_map/all_to_all | solution.py:686
  111.1 6.6 %backward.7 = (bf16[3072,128]{1,0:T(8,128)(2,1)S(1)}, bf16[576,2048]{1,0:T(8,128)(2,1)}, bf16[576,512]{1,0:T(8,128)(2,1)S(1)}, bf16[576,512]{1,0:T(8,128)(2,1)S(1)}) custom-call(s32[3]{0:T(128)S(1)} %pad_add_fusion.4.info_ref, bf16[32,96,128]{2,1,0:T(8,128)(2,1)S(1)} %all-to-all-done.2.got_hbm, ...), custom_call_target="tpu_custom_call", output_to_operand_aliasing={{1}: (7, {}), {2}: (8, {}), {3}: (9, {})} | custom-call | flops 1207959552 | bytes 12000000 | tf_op jit(solution)/shard_map/backward/pallas_call | solution.py:536
  118.7 3.9 %all-to-all-start.4 = ((bf16[32,96,128]{2,1,0:T(8,128)(2,1)}), bf16[32,96,128]{2,1,0:T(8,128)(2,1)S(1)}, u32[]{:S(2)}, u32[]{:S(2)}) async-start(bf16[32,96,128]{2,1,0:T(8,128)(2,1)} %bitcast.58), calls=%async_computation.4 | async-start | bytes 1572864 | tf_op jit(solution)/shard_map/all_to_all | solution.py:686
  122.6 4.1 %dispatch.9 = bf16[3072,128]{1,0:T(8,128)(2,1)} custom-call(s32[3]{0:T(128)S(1)} %copy-done.20, s32[576]{0:T(1024)S(1)} %copy-done.14, f32[576]{0:T(1024)S(1)} %copy-done.13, bf16[3,64,2048]{2,1,0:T(8,128)(2,1)} %bitcast.86), custom_call_target="tpu_custom_call" | custom-call | flops 1000000 | bytes 4000000 | tf_op jit(solution)/shard_map/dispatch/pallas_call | solution.py:149
  126.7 10.1 %all-to-all-done.4 = bf16[32,96,128]{2,1,0:T(8,128)(2,1)S(1)} async-done(((bf16[32,96,128]{2,1,0:T(8,128)(2,1)}), bf16[32,96,128]{2,1,0:T(8,128)(2,1)S(1)}, u32[]{:S(2)}, u32[]{:S(2)}) %all-to-all-start.4) | async-done | bytes 786464 | tf_op jit(solution)/shard_map/all_to_all | solution.py:686
  136.8 1.4 combine.7.new_ref
  138.3 3.8 %all-to-all-start.6 = ((bf16[32,96,128]{2,1,0:T(8,128)(2,1)}), bf16[32,96,128]{2,1,0:T(8,128)(2,1)S(1)}, u32[]{:S(2)}, u32[]{:S(2)}) async-start(bf16[32,96,128]{2,1,0:T(8,128)(2,1)} %bitcast.26), calls=%async_computation.6 | async-start | bytes 1572864 | tf_op jit(solution)/shard_map/all_to_all | solution.py:686
  142.1 1.3 collective-permute-start.1
  143.5 2.5 keep_rows.6.refs_0_
  145.9 5.7 %collective-permute-done.1.refs_1_ = bf16[1024,128]{1,0:T(8,128)(2,1)S(1)} collective-permute-done((bf16[1024,128]{1,0:T(8,128)(2,1)S(1)}, bf16[1024,128]{1,0:T(8,128)(2,1)S(1)}, u32[]{:S(2)}, u32[]{:S(2)}) %collective-permute-start.1) | collective-permute-done | bytes 262176 | tf_op jit(solution)/shard_map/ppermute | solution.py:746
  151.6 2.8 dispatch.10
  154.4 1.9 all-to-all-done.6.got_hbm
  156.3 6.2 %all-to-all-start.5 = ((bf16[32,96,128]{2,1,0:T(8,128)(2,1)}), bf16[32,96,128]{2,1,0:T(8,128)(2,1)S(1)}, u32[]{:S(2)}, u32[]{:S(2)}) async-start(bf16[32,96,128]{2,1,0:T(8,128)(2,1)} %bitcast.25), calls=%async_computation.5 | async-start | bytes 1572864 | tf_op jit(solution)/shard_map/all_to_all | solution.py:686
  162.5 4.8 %forward.5 = (bf16[576,2048]{1,0:T(8,128)(2,1)}, bf16[192,512]{1,0:T(8,128)(2,1)}, f32[2,192,512]{2,1,0:T(8,128)}) custom-call(bf16[32,96,128]{2,1,0:T(8,128)(2,1)} %copy-done.23, bf16[2048,512]{1,0:T(8,128)(2,1)} %bitcast.63, bf16[2048,512]{1,0:T(8,128)(2,1)} %bitcast.72, bf16[576,2048]{1,0:T(8,128)(2,1)} %get-tuple-element.75.refs_0_), custom_call_target="tpu_custom_call", output_to_operand_aliasing={{0}: (3, {})} | custom-call | flops 805306368 | bytes 8000000 | tf_op jit(solution)/shard_map/forward/pallas_call | solution.py:428
  167.4 9.4 %all-to-all-done.5.got_hbm = bf16[32,96,128]{2,1,0:T(8,128)(2,1)S(1)} async-done(((bf16[32,96,128]{2,1,0:T(8,128)(2,1)}), bf16[32,96,128]{2,1,0:T(8,128)(2,1)S(1)}, u32[]{:S(2)}, u32[]{:S(2)}) %all-to-all-start.5) | async-done | bytes 786464 | tf_op jit(solution)/shard_map/all_to_all | solution.py:686
  176.7 6.4 %backward.8 = (bf16[3072,128]{1,0:T(8,128)(2,1)}, bf16[576,2048]{1,0:T(8,128)(2,1)}, bf16[576,512]{1,0:T(8,128)(2,1)S(1)}, bf16[576,512]{1,0:T(8,128)(2,1)S(1)}) custom-call(s32[3]{0:T(128)S(1)} %pad_add_fusion.3.info_ref, bf16[32,96,128]{2,1,0:T(8,128)(2,1)S(1)} %all-to-all-done.5.got_hbm, ...), custom_call_target="tpu_custom_call", output_to_operand_aliasing={{1}: (8, {}), {2}: (9, {}), {3}: (10, {})} | custom-call | flops 1207959552 | bytes 12000000 | tf_op jit(solution)/shard_map/backward/pallas_call | solution.py:536
  183.2 3.8 %all-to-all-start.7 = ((bf16[32,96,128]{2,1,0:T(8,128)(2,1)}), bf16[32,96,128]{2,1,0:T(8,128)(2,1)S(1)}, u32[]{:S(2)}, u32[]{:S(2)}) async-start(bf16[32,96,128]{2,1,0:T(8,128)(2,1)} %bitcast.27), calls=%async_computation.7 | async-start | bytes 1572864 | tf_op jit(solution)/shard_map/all_to_all | solution.py:686
  187.0 12.1 %root_start.1.state_in = f32[2,512,512]{2,1,0:T(8,128)} custom-call(bf16[192,512]{1,0:T(8,128)(2,1)} %copy-done.21, bf16[192,512]{1,0:T(8,128)(2,1)} %get-tuple-element.82.refs_1_, bf16[192,512]{1,0:T(8,128)(2,1)} %get-tuple-element.83.refs_2_), custom_call_target="tpu_custom_call" | custom-call | flops 6442450944 | bytes 4000000 | tf_op jit(solution)/shard_map/root_start/pallas_call | solution.py:659
  199.1 2.1 all-to-all-done.7
  201.2 1.4 combine.8.new_ref
  204.1 2.5 keep_rows.7.refs_0_
  206.5 6.7 %collective-permute-done.2.refs_0_ = bf16[1024,128]{1,0:T(8,128)(2,1)S(1)} collective-permute-done((bf16[1024,128]{1,0:T(8,128)(2,1)S(1)}, bf16[1024,128]{1,0:T(8,128)(2,1)S(1)}, u32[]{:S(2)}, u32[]{:S(2)}) %collective-permute-start.2) | collective-permute-done | bytes 262176 | tf_op jit(solution)/shard_map/ppermute | solution.py:746
  213.2 1.9 dispatch.11
  215.2 19.4 %all_to_all.70.got_hbm = bf16[32,96,128]{2,1,0:T(8,128)(2,1)S(1)} all-to-all(bf16[32,96,128]{2,1,0:T(8,128)(2,1)S(1)} %bitcast.56), channel_id=1, replica_groups=mesh['section'=4,'expert'=32] {'expert'}, dimensions={0} | all-to-all | bytes 1572864 | tf_op jit(solution)/shard_map/all_to_all | solution.py:686
  234.6 6.9 %backward.9 = (bf16[3072,128]{1,0:T(8,128)(2,1)}, bf16[576,2048]{1,0:T(8,128)(2,1)}, bf16[576,512]{1,0:T(8,128)(2,1)S(1)}, bf16[576,512]{1,0:T(8,128)(2,1)S(1)}) custom-call(s32[3]{0:T(128)S(1)} %pad_add_fusion.2.info_ref, bf16[32,96,128]{2,1,0:T(8,128)(2,1)S(1)} %all_to_all.70.got_hbm, ...), custom_call_target="tpu_custom_call", output_to_operand_aliasing={{1}: (8, {}), {2}: (9, {}), {3}: (10, {})} | custom-call | flops 1207959552 | bytes 12000000 | tf_op jit(solution)/shard_map/backward/pallas_call | solution.py:536
  241.5 3.8 %all-to-all-start.9 = ((bf16[32,96,128]{2,1,0:T(8,128)(2,1)}), bf16[32,96,128]{2,1,0:T(8,128)(2,1)S(1)}, u32[]{:S(2)}, u32[]{:S(2)}) async-start(bf16[32,96,128]{2,1,0:T(8,128)(2,1)} %bitcast.30), calls=%async_computation.9 | async-start | bytes 1572864 | tf_op jit(solution)/shard_map/all_to_all | solution.py:686
  245.3 11.5 %root_more.1.state_in = f32[2,512,512]{2,1,0:T(8,128)} custom-call(f32[2,512,512]{2,1,0:T(8,128)} %root_start.1.state_in), custom_call_target="tpu_custom_call" | custom-call | flops 6442450944 | bytes 4000000 | tf_op jit(solution)/shard_map/root_more/pallas_call | solution.py:659
  256.8 2.7 all-to-all-done.9
  259.5 1.4 combine.9.new_ref
  262.4 2.8 keep_rows.8.refs_0_
  265.2 5.7 %collective-permute-done.3.refs_0_ = bf16[1024,128]{1,0:T(8,128)(2,1)S(1)} collective-permute-done((bf16[1024,128]{1,0:T(8,128)(2,1)S(1)}, bf16[1024,128]{1,0:T(8,128)(2,1)S(1)}, u32[]{:S(2)}, u32[]{:S(2)}) %collective-permute-start.3) | collective-permute-done | bytes 262176 | tf_op jit(solution)/shard_map/ppermute | solution.py:746
  270.8 1.9 dispatch.12
  272.7 19.1 %all_to_all.71.got_hbm = bf16[32,96,128]{2,1,0:T(8,128)(2,1)S(1)} all-to-all(bf16[32,96,128]{2,1,0:T(8,128)(2,1)S(1)} %bitcast.57), channel_id=1, replica_groups=mesh['section'=4,'expert'=32] {'expert'}, dimensions={0} | all-to-all | bytes 1572864 | tf_op jit(solution)/shard_map/all_to_all | solution.py:686
  291.8 7.1 %backward.10 = (bf16[3072,128]{1,0:T(8,128)(2,1)}, bf16[576,2048]{1,0:T(8,128)(2,1)}, bf16[576,512]{1,0:T(8,128)(2,1)S(1)}, bf16[576,512]{1,0:T(8,128)(2,1)S(1)}) custom-call(s32[3]{0:T(128)S(1)} %pad_add_fusion.1.info_ref, bf16[32,96,128]{2,1,0:T(8,128)(2,1)S(1)} %all_to_all.71.got_hbm, ...), custom_call_target="tpu_custom_call", output_to_operand_aliasing={{1}: (8, {}), {2}: (9, {}), {3}: (10, {})} | custom-call | flops 1207959552 | bytes 12000000 | tf_op jit(solution)/shard_map/backward/pallas_call | solution.py:536
  299.0 3.8 %all-to-all-start.11 = ((bf16[32,96,128]{2,1,0:T(8,128)(2,1)}), bf16[32,96,128]{2,1,0:T(8,128)(2,1)S(1)}, u32[]{:S(2)}, u32[]{:S(2)}) async-start(bf16[32,96,128]{2,1,0:T(8,128)(2,1)} %bitcast.33), calls=%async_computation.11 | async-start | bytes 1572864 | tf_op jit(solution)/shard_map/all_to_all | solution.py:686
  302.8 4.8 %root_end.1.lead_ref = bf16[512,576]{1,0:T(8,128)(2,1)} custom-call(f32[2,512,512]{2,1,0:T(8,128)} %root_more.1.state_in, bf16[192,512]{1,0:T(8,128)(2,1)} %copy-done.21, bf16[192,512]{1,0:T(8,128)(2,1)} %get-tuple-element.82.refs_1_, bf16[192,512]{1,0:T(8,128)(2,1)} %get-tuple-element.83.refs_2_), custom_call_target="tpu_custom_call" | custom-call | flops 2415919104 | bytes 4000000 | tf_op jit(solution)/shard_map/root_end/pallas_call | solution.py:659
  307.6 9.4 %all-to-all-done.11 = bf16[32,96,128]{2,1,0:T(8,128)(2,1)S(1)} async-done(((bf16[32,96,128]{2,1,0:T(8,128)(2,1)}), bf16[32,96,128]{2,1,0:T(8,128)(2,1)S(1)}, u32[]{:S(2)}, u32[]{:S(2)}) %all-to-all-start.11) | async-done | bytes 786464 | tf_op jit(solution)/shard_map/all_to_all | solution.py:686
  317.0 1.4 combine.10.new_ref
  319.8 2.8 keep_rows.9.refs_2_
  322.6 5.7 %collective-permute-done.4.refs_0_ = bf16[1024,128]{1,0:T(8,128)(2,1)S(1)} collective-permute-done((bf16[1024,128]{1,0:T(8,128)(2,1)S(1)}, bf16[1024,128]{1,0:T(8,128)(2,1)S(1)}, u32[]{:S(2)}, u32[]{:S(2)}) %collective-permute-start.4) | collective-permute-done | bytes 262176 | tf_op jit(solution)/shard_map/ppermute | solution.py:746
  328.3 1.9 dispatch.13
  330.2 18.2 %all_to_all.72.got_hbm = bf16[32,96,128]{2,1,0:T(8,128)(2,1)S(1)} all-to-all(bf16[32,96,128]{2,1,0:T(8,128)(2,1)S(1)} %bitcast.55), channel_id=1, replica_groups=mesh['section'=4,'expert'=32] {'expert'}, dimensions={0} | all-to-all | bytes 1572864 | tf_op jit(solution)/shard_map/all_to_all | solution.py:686
  348.5 6.9 %backward.11 = (bf16[3072,128]{1,0:T(8,128)(2,1)}, bf16[576,2048]{1,0:T(8,128)(2,1)}, bf16[576,512]{1,0:T(8,128)(2,1)S(1)}, bf16[576,512]{1,0:T(8,128)(2,1)S(1)}) custom-call(s32[3]{0:T(128)S(1)} %pad_add_fusion.info_ref, bf16[32,96,128]{2,1,0:T(8,128)(2,1)S(1)} %all_to_all.72.got_hbm, ...), custom_call_target="tpu_custom_call", output_to_operand_aliasing={{1}: (8, {}), {2}: (9, {}), {3}: (10, {})} | custom-call | flops 1207959552 | bytes 12000000 | tf_op jit(solution)/shard_map/backward/pallas_call | solution.py:536
  355.4 3.8 %all-to-all-start.13 = ((bf16[32,96,128]{2,1,0:T(8,128)(2,1)}), bf16[32,96,128]{2,1,0:T(8,128)(2,1)S(1)}, u32[]{:S(2)}, u32[]{:S(2)}) async-start(bf16[32,96,128]{2,1,0:T(8,128)(2,1)} %bitcast.36), calls=%async_computation.13 | async-start | bytes 1572864 | tf_op jit(solution)/shard_map/all_to_all | solution.py:686
  359.2 10.7 %gradients.1 = (f32[2048,512]{1,0:T(8,128)}, f32[2048,512]{1,0:T(8,128)}, f32[512,2048]{1,0:T(8,128)}) custom-call(bf16[512,576]{1,0:T(8,128)(2,1)} %root_end.1.lead_ref, bf16[576,512]{1,0:T(8,128)(2,1)} %copy-done.4, bf16[576,512]{1,0:T(8,128)(2,1)} %copy-done.5, bf16[576,2048]{1,0:T(8,128)(2,1)} %get-tuple-element.111.xs_ref, ...), custom_call_target="tpu_custom_call" | custom-call | flops 3623878656 | bytes 18000000 | tf_op jit(solution)/shard_map/gradients/pallas_call | solution.py:358
  369.9 3.5 all-to-all-done.13
  373.4 3.0 combine.11
  (80 shorter events, 9.4 us)
Async XLA Ops:
  2.8 6.3 %copy-start.24 = (s32[3,128]{1,0:T(4,128)}, s32[3,128]{1,0:T(4,128)S(1)}, u32[]{:S(2)}) copy-start(s32[3,128]{1,0:T(4,128)S(1)} %convert_reduce_fusion) | copy-start | bytes 4612
  9.1 32.3 %all-to-all-start = ((bf16[32,192,128]{2,1,0:T(8,128)(2,1)}), bf16[32,192,128]{2,1,0:T(8,128)(2,1)S(1)}, u32[]{:S(2)}, u32[]{:S(2)}) async-start(bf16[32,192,128]{2,1,0:T(8,128)(2,1)} %bitcast.87), calls=%async_computation | async-start | bytes 3145728 | tf_op jit(solution)/shard_map/all_to_all | solution.py:686
  18.8 52.2 %copy-start.19 = (s32[3]{0:T(128)}, s32[3]{0:T(128)S(1)}, u32[]{:S(2)}) copy-start(s32[3]{0:T(128)S(1)} %pad_add_fusion.5.info_ref) | copy-start | bytes 40
  41.4 4.5 %copy-start.6 = (bf16[32,192,128]{2,1,0:T(8,128)(2,1)}, bf16[32,192,128]{2,1,0:T(8,128)(2,1)S(1)}, u32[]{:S(2)}) copy-start(bf16[32,192,128]{2,1,0:T(8,128)(2,1)S(1)} %all-to-all-done.got_hbm) | copy-start | bytes 4718596
  45.9 6.5 %copy-start = (f32[2,192,512]{2,1,0:T(8,128)}, f32[2,192,512]{2,1,0:T(8,128)S(1)}, u32[]{:S(2)}) copy-start(f32[2,192,512]{2,1,0:T(8,128)S(1)} %get-tuple-element.60.refs_0_) | copy-start | bytes 2359300
  45.9 6.5 %copy-start.21 = (bf16[192,512]{1,0:T(8,128)(2,1)}, bf16[192,512]{1,0:T(8,128)(2,1)S(1)}, u32[]{:S(2)}) copy-start(bf16[192,512]{1,0:T(8,128)(2,1)S(1)} %get-tuple-element.81.refs_0_) | copy-start | bytes 589828
  45.9 10.7 %copy-start.26 = (s32[1,3,64,2]{2,3,1,0:T(2,128)S(1)}, s32[1,3,64,2]{2,3,1,0:T(2,128)}, u32[]{:S(2)}) copy-start(s32[1,3,64,2]{2,3,1,0:T(2,128)} %param.11) | copy-start | bytes 4612
  45.9 11.0 %copy-start.13 = (f32[576]{0:T(1024)S(1)}, f32[576]{0:T(1024)}, u32[]{:S(2)}) copy-start(f32[576]{0:T(1024)} %reshape.116.scale_ref) | copy-start | bytes 6916
  45.9 11.0 %copy-start.14 = (s32[576]{0:T(1024)S(1)}, s32[576]{0:T(1024)}, u32[]{:S(2)}) copy-start(s32[576]{0:T(1024)} %reshape.115.src_ref) | copy-start | bytes 6916
  52.4 8.7 %copy-start.25 = (s32[3,128]{1,0:T(4,128)S(1)}, s32[3,128]{1,0:T(4,128)}, u32[]{:S(2)}) copy-start(s32[3,128]{1,0:T(4,128)} %copy-done.24) | copy-start | bytes 4612
  52.4 18.6 %copy-start.1 = (bf16[3,64,2048]{2,1,0:T(8,128)(2,1)S(1)}, bf16[3,64,2048]{2,1,0:T(8,128)(2,1)}, u32[]{:S(2)}) copy-start(bf16[3,64,2048]{2,1,0:T(8,128)(2,1)} %refs_0_.9) | copy-start | bytes 2359300
  52.4 18.6 %all-to-all-start.1 = ((bf16[32,96,128]{2,1,0:T(8,128)(2,1)}), bf16[32,96,128]{2,1,0:T(8,128)(2,1)S(1)}, u32[]{:S(2)}, u32[]{:S(2)}) async-start(bf16[32,96,128]{2,1,0:T(8,128)(2,1)} %bitcast.19), calls=%async_computation.1 | async-start | bytes 1572864 | tf_op jit(solution)/shard_map/all_to_all | solution.py:686
  72.7 5.2 %copy-start.8 = (bf16[1024,128]{1,0:T(8,128)(2,1)}, bf16[1024,128]{1,0:T(8,128)(2,1)S(1)}, u32[]{:S(2)}) copy-start(bf16[1024,128]{1,0:T(8,128)(2,1)S(1)} %combine.6.new_ref) | copy-start | bytes 786436
  72.7 18.0 %all-to-all-start.3 = ((bf16[32,96,128]{2,1,0:T(8,128)(2,1)}), bf16[32,96,128]{2,1,0:T(8,128)(2,1)S(1)}, u32[]{:S(2)}, u32[]{:S(2)}) async-start(bf16[32,96,128]{2,1,0:T(8,128)(2,1)} %bitcast.22), calls=%async_computation.3 | async-start | bytes 1572864 | tf_op jit(solution)/shard_map/all_to_all | solution.py:686
  76.5 9.5 %collective-permute-start = (bf16[1024,128]{1,0:T(8,128)(2,1)S(1)}, bf16[1024,128]{1,0:T(8,128)(2,1)S(1)}, u32[]{:S(2)}, u32[]{:S(2)}) collective-permute-start(bf16[1024,128]{1,0:T(8,128)(2,1)S(1)} %combine.6.new_ref), channel_id=1, source_target_pairs={{32,0},{64,32},{96,64},{33,1},{65,33},{97,65},{34,2},{66,34},{98,6... | collective-permute-start | bytes 786440 | tf_op jit(solution)/shard_map/ppermute | solution.py:746
  77.9 59.0 %copy-start.17 = (s32[3]{0:T(128)}, s32[3]{0:T(128)S(1)}, u32[]{:S(2)}) copy-start(s32[3]{0:T(128)S(1)} %pad_add_fusion.4.info_ref) | copy-start | bytes 40
  90.7 6.2 %copy-start.22 = (bf16[32,96,128]{2,1,0:T(8,128)(2,1)}, bf16[32,96,128]{2,1,0:T(8,128)(2,1)S(1)}, u32[]{:S(2)}) copy-start(bf16[32,96,128]{2,1,0:T(8,128)(2,1)S(1)} %all-to-all-done.3.got_hbm) | copy-start | bytes 2359300
  90.7 20.4 %all-to-all-start.2 = ((bf16[32,96,128]{2,1,0:T(8,128)(2,1)}), bf16[32,96,128]{2,1,0:T(8,128)(2,1)S(1)}, u32[]{:S(2)}, u32[]{:S(2)}) async-start(bf16[32,96,128]{2,1,0:T(8,128)(2,1)} %bitcast.21), calls=%async_computation.2 | async-start | bytes 1572864 | tf_op jit(solution)/shard_map/all_to_all | solution.py:686
  111.1 11.5 %copy-start.20 = (s32[3]{0:T(128)S(1)}, s32[3]{0:T(128)}, u32[]{:S(2)}) copy-start(s32[3]{0:T(128)} %constant.40.clone.info_ref) | copy-start | bytes 40
  117.8 0.9 copy-start.12
  118.7 18.2 %copy-start.2 = (bf16[3,64,2048]{2,1,0:T(8,128)(2,1)S(1)}, bf16[3,64,2048]{2,1,0:T(8,128)(2,1)}, u32[]{:S(2)}) copy-start(bf16[3,64,2048]{2,1,0:T(8,128)(2,1)} %refs_0_.9) | copy-start | bytes 2359300
  118.7 18.2 %all-to-all-start.4 = ((bf16[32,96,128]{2,1,0:T(8,128)(2,1)}), bf16[32,96,128]{2,1,0:T(8,128)(2,1)S(1)}, u32[]{:S(2)}, u32[]{:S(2)}) async-start(bf16[32,96,128]{2,1,0:T(8,128)(2,1)} %bitcast.58), calls=%async_computation.4 | async-start | bytes 1572864 | tf_op jit(solution)/shard_map/all_to_all | solution.py:686
  138.3 5.2 %copy-start.10 = (bf16[1024,128]{1,0:T(8,128)(2,1)}, bf16[1024,128]{1,0:T(8,128)(2,1)S(1)}, u32[]{:S(2)}) copy-start(bf16[1024,128]{1,0:T(8,128)(2,1)S(1)} %combine.7.new_ref) | copy-start | bytes 786436
  138.3 18.0 %all-to-all-start.6 = ((bf16[32,96,128]{2,1,0:T(8,128)(2,1)}), bf16[32,96,128]{2,1,0:T(8,128)(2,1)S(1)}, u32[]{:S(2)}, u32[]{:S(2)}) async-start(bf16[32,96,128]{2,1,0:T(8,128)(2,1)} %bitcast.26), calls=%async_computation.6 | async-start | bytes 1572864 | tf_op jit(solution)/shard_map/all_to_all | solution.py:686
  142.1 9.5 %collective-permute-start.1 = (bf16[1024,128]{1,0:T(8,128)(2,1)S(1)}, bf16[1024,128]{1,0:T(8,128)(2,1)S(1)}, u32[]{:S(2)}, u32[]{:S(2)}) collective-permute-start(bf16[1024,128]{1,0:T(8,128)(2,1)S(1)} %combine.7.new_ref), channel_id=1, source_target_pairs={{32,0},{64,32},{96,64},{33,1},{65,33},{97,65},{34,2},{66,34},{98,6... | collective-permute-start | bytes 786440 | tf_op jit(solution)/shard_map/ppermute | solution.py:746
  143.5 57.7 %copy-start.18 = (s32[3]{0:T(128)}, s32[3]{0:T(128)S(1)}, u32[]{:S(2)}) copy-start(s32[3]{0:T(128)S(1)} %pad_add_fusion.3.info_ref) | copy-start | bytes 40
  156.3 6.2 %copy-start.23 = (bf16[32,96,128]{2,1,0:T(8,128)(2,1)}, bf16[32,96,128]{2,1,0:T(8,128)(2,1)S(1)}, u32[]{:S(2)}) copy-start(bf16[32,96,128]{2,1,0:T(8,128)(2,1)S(1)} %all-to-all-done.6.got_hbm) | copy-start | bytes 2359300
  156.3 20.4 %all-to-all-start.5 = ((bf16[32,96,128]{2,1,0:T(8,128)(2,1)}), bf16[32,96,128]{2,1,0:T(8,128)(2,1)S(1)}, u32[]{:S(2)}, u32[]{:S(2)}) async-start(bf16[32,96,128]{2,1,0:T(8,128)(2,1)} %bitcast.25), calls=%async_computation.5 | async-start | bytes 1572864 | tf_op jit(solution)/shard_map/all_to_all | solution.py:686
  183.2 18.0 %all-to-all-start.7 = ((bf16[32,96,128]{2,1,0:T(8,128)(2,1)}), bf16[32,96,128]{2,1,0:T(8,128)(2,1)S(1)}, u32[]{:S(2)}, u32[]{:S(2)}) async-start(bf16[32,96,128]{2,1,0:T(8,128)(2,1)} %bitcast.27), calls=%async_computation.7 | async-start | bytes 1572864 | tf_op jit(solution)/shard_map/all_to_all | solution.py:686
  187.0 14.2 %copy-start.3 = (bf16[3,64,2048]{2,1,0:T(8,128)(2,1)S(1)}, bf16[3,64,2048]{2,1,0:T(8,128)(2,1)}, u32[]{:S(2)}) copy-start(bf16[3,64,2048]{2,1,0:T(8,128)(2,1)} %refs_0_.9) | copy-start | bytes 2359300
  202.7 1.4 copy-start.11
  202.7 10.6 %collective-permute-start.2 = (bf16[1024,128]{1,0:T(8,128)(2,1)S(1)}, bf16[1024,128]{1,0:T(8,128)(2,1)S(1)}, u32[]{:S(2)}, u32[]{:S(2)}) collective-permute-start(bf16[1024,128]{1,0:T(8,128)(2,1)S(1)} %combine.8.new_ref), channel_id=1, source_target_pairs={{32,0},{64,32},{96,64},{33,1},{65,33},{97,65},{34,2},{66,34},{98,6... | collective-permute-start | bytes 786440 | tf_op jit(solution)/shard_map/ppermute | solution.py:746
  204.1 55.5 %copy-start.16 = (s32[3]{0:T(128)}, s32[3]{0:T(128)S(1)}, u32[]{:S(2)}) copy-start(s32[3]{0:T(128)S(1)} %pad_add_fusion.2.info_ref) | copy-start | bytes 40
  241.5 18.0 %all-to-all-start.9 = ((bf16[32,96,128]{2,1,0:T(8,128)(2,1)}), bf16[32,96,128]{2,1,0:T(8,128)(2,1)S(1)}, u32[]{:S(2)}, u32[]{:S(2)}) async-start(bf16[32,96,128]{2,1,0:T(8,128)(2,1)} %bitcast.30), calls=%async_computation.9 | async-start | bytes 1572864 | tf_op jit(solution)/shard_map/all_to_all | solution.py:686
  261.0 1.4 copy-start.9
  261.0 9.8 %collective-permute-start.3 = (bf16[1024,128]{1,0:T(8,128)(2,1)S(1)}, bf16[1024,128]{1,0:T(8,128)(2,1)S(1)}, u32[]{:S(2)}, u32[]{:S(2)}) collective-permute-start(bf16[1024,128]{1,0:T(8,128)(2,1)S(1)} %combine.9.new_ref), channel_id=1, source_target_pairs={{32,0},{64,32},{96,64},{33,1},{65,33},{97,65},{34,2},{66,34},{98,6... | collective-permute-start | bytes 786440 | tf_op jit(solution)/shard_map/ppermute | solution.py:746
  262.4 54.7 %copy-start.15 = (s32[3]{0:T(128)}, s32[3]{0:T(128)S(1)}, u32[]{:S(2)}) copy-start(s32[3]{0:T(128)S(1)} %pad_add_fusion.1.info_ref) | copy-start | bytes 40
  299.0 18.1 %all-to-all-start.11 = ((bf16[32,96,128]{2,1,0:T(8,128)(2,1)}), bf16[32,96,128]{2,1,0:T(8,128)(2,1)S(1)}, u32[]{:S(2)}, u32[]{:S(2)}) async-start(bf16[32,96,128]{2,1,0:T(8,128)(2,1)} %bitcast.33), calls=%async_computation.11 | async-start | bytes 1572864 | tf_op jit(solution)/shard_map/all_to_all | solution.py:686
  318.4 1.4 copy-start.7
  318.4 9.8 %collective-permute-start.4 = (bf16[1024,128]{1,0:T(8,128)(2,1)S(1)}, bf16[1024,128]{1,0:T(8,128)(2,1)S(1)}, u32[]{:S(2)}, u32[]{:S(2)}) collective-permute-start(bf16[1024,128]{1,0:T(8,128)(2,1)S(1)} %combine.10.new_ref), channel_id=1, source_target_pairs={{32,0},{64,32},{96,64},{33,1},{65,33},{97,65},{34,2},{66,34},{98,6... | collective-permute-start | bytes 786440 | tf_op jit(solution)/shard_map/ppermute | solution.py:746
  355.4 3.8 %copy-start.4 = (bf16[576,512]{1,0:T(8,128)(2,1)}, bf16[576,512]{1,0:T(8,128)(2,1)S(1)}, u32[]{:S(2)}) copy-start(bf16[576,512]{1,0:T(8,128)(2,1)S(1)} %get-tuple-element.109.dg_ref) | copy-start | bytes 1769476
  355.4 3.8 %copy-start.5 = (bf16[576,512]{1,0:T(8,128)(2,1)}, bf16[576,512]{1,0:T(8,128)(2,1)S(1)}, u32[]{:S(2)}) copy-start(bf16[576,512]{1,0:T(8,128)(2,1)S(1)} %get-tuple-element.110.du_ref) | copy-start | bytes 1769476
  355.4 18.0 %all-to-all-start.13 = ((bf16[32,96,128]{2,1,0:T(8,128)(2,1)}), bf16[32,96,128]{2,1,0:T(8,128)(2,1)S(1)}, u32[]{:S(2)}, u32[]{:S(2)}) async-start(bf16[32,96,128]{2,1,0:T(8,128)(2,1)} %bitcast.36), calls=%async_computation.13 | async-start | bytes 1572864 | tf_op jit(solution)/shard_map/all_to_all | solution.py:686
